TPU v7x, 256 devices: a whole 4x4x8 slice. The times are simulated.
256 devices in a mesh: dp: 4 (over x), table: 64 (over y, z, core).
Axes of the slice: x: 4, y: 4, z: 8, core: 2. Of those that a mesh axis runs over, the one named last changes fastest.
Arguments:
- shard_of: int32 [2048, 200, 3], P(('dp', 'table')), may hold values from 0 to 63, all different within a row; in each aligned block of 1600 rows (0 to 1599, 1600 to 3199, ..., all dimensions but the last counted through in order) at most 152 rows name the same one
- offsets: int32 [2048, 200, 3], P(('dp', 'table')), may hold values from 0 to 2047
- table: bfloat16 [3, 131072, 256], P(None, 'table'), may hold values from -4 to 4
- weight_one: bfloat16 [768, 256], replicated, may hold values from -0.21875 to 0.21875
- gain_one: float32 [256], replicated, may hold values from 0.5 to 1.5
- weight_two: bfloat16 [768, 256], replicated, may hold values from -0.21875 to 0.21875
- gain_two: float32 [256], replicated, may hold values from 0.5 to 1.5
- grad_out: bfloat16 [2048, 200, 256], P(('dp', 'table')), may hold values from -6 to 6
Outputs:
- block_out: bfloat16 [2048, 200, 256], P(('dp', 'table'))
- grad_weight_one: float32 [768, 256], replicated
- grad_weight_two: float32 [768, 256], replicated
- grad_gain_one: float32 [256], replicated
- grad_gain_two: float32 [256], replicated
- table_grad: float32 [3, 131072, 256], P(None, 'table', 'dp')
Inputs may be any that keep to these rules, and one draw needn't show every extreme that they name: `shard_of`: the three lookups of one item go to three different shards; at most 152 lookups of the items of one device go to one shard, and exactly 152 for some shard of some device.
All inputs are finite; a program needn't handle non-finite values.
Results may differ from a plain program's by a relative error of at most 0.017.
Values may be sent and summed in bfloat16 or wider, within the bound.
A program may use at most 128 MiB of HBM per device.

v0:
```python
import functools
import math

import jax
import jax.numpy as jnp
from jax import lax
from jax.experimental import pallas as pl
from jax.experimental.pallas import tpu as pltpu
from jax.sharding import PartitionSpec as P

F32, BF16, I32 = jnp.float32, jnp.bfloat16, jnp.int32
MESH = pl.DeviceIdType.MESH
GELU_C = 0.7978845608028654
GELU_K = 0.044715
GROUP = 8
AXES = (("dp", 4, 1), ("table", 4, 16), ("table", 8, 2), ("table", 2, 1))


def gelu_parts(inputs):
    inner = GELU_C * (inputs + GELU_K * inputs * inputs * inputs)
    tangent = jnp.tanh(inner)
    output = 0.5 * inputs * (1.0 + tangent)
    slope = 0.5 * (1.0 + tangent) + 0.5 * inputs * (1.0 - tangent * tangent) * GELU_C * (
        1.0 + 3.0 * GELU_K * inputs * inputs
    )
    return (output, slope)


def index_kernel(shards, cap, rows_dev, sh_ref, off_ref, place_ref, req_ref, item_ref):
    tables, sessions, length = sh_ref.shape
    tri = (
        lax.broadcasted_iota(I32, (length, length), 0) < lax.broadcasted_iota(I32, (length, length), 1)
    ).astype(BF16)
    lane = lax.broadcasted_iota(I32, (1, length), 1)
    shard_id = lax.broadcasted_iota(I32, (shards, length), 0)
    slot_id = lax.broadcasted_iota(I32, (cap, length), 0)
    base = jnp.zeros((shards, 1), F32)
    listed = [jnp.zeros((shards, cap), F32) for _ in range(4)]
    dims = (((1,), (1,)), ((), ()))
    for t in range(tables):
        for s in range(sessions):
            sh = sh_ref[t, s : s + 1, :]
            code = off_ref[t, s : s + 1, :] + (t * rows_dev + 1)
            item = lane + s * length
            hit = shard_id == sh
            hot = jnp.where(hit, 1.0, 0.0)
            hot16 = hot.astype(BF16)
            prefix = jnp.dot(hot16, tri, preferred_element_type=F32) + base
            rank = jnp.sum(jnp.where(hit, prefix, 0.0), axis=0, keepdims=True).astype(I32)
            base = base + jnp.sum(hot, axis=1, keepdims=True)
            place_ref[t, s : s + 1, :] = sh * cap + rank
            here = slot_id == rank
            for n, digit in enumerate((code // 256, code % 256, item // 256, item % 256)):
                listed[n] += lax.dot_general(
                    hot16,
                    jnp.where(here, digit.astype(F32), 0.0).astype(BF16),
                    dims,
                    preferred_element_type=F32,
                )
    req_ref[...] = (listed[0] * 256.0 + listed[1]).astype(I32)
    item_ref[...] = (listed[2] * 256.0 + listed[3]).astype(I32)


def make_index(sh, off, shards, cap, rows_dev):
    block = jax.ShapeDtypeStruct((shards, cap), I32)
    return pl.pallas_call(
        functools.partial(index_kernel, shards, cap, rows_dev),
        out_shape=(jax.ShapeDtypeStruct(sh.shape, I32), block, block),
        cost_estimate=pl.CostEstimate(flops=10**9, bytes_accessed=10**6, transcendentals=0),
        name="index",
    )(sh, off)


def whole(shape):
    zeros = (0,) * len(shape)
    return pl.BlockSpec(shape, lambda b, i: zeros, pipeline_mode=pl.Buffered(1))


def widen(src, dst, rows, at=0):
    values = src[pl.ds(at, rows), :].astype(F32)
    dst[pl.ds(2 * at, rows, stride=2), :] = values[:, :128]
    dst[pl.ds(2 * at + 1, rows, stride=2), :] = values[:, 128:]


def pair(index):
    return pl.ds(pl.multiple_of(2 * index, 2), 2)


PAD = 8


def padded(values, length):
    zeros = jnp.zeros((PAD, values.shape[1]), F32)
    parts = []
    for start in range(0, values.shape[0], length):
        parts += [zeros, values[start : start + length]]
    return jnp.concatenate(parts, axis=0)


def unpadded(values, length):
    pitch = length + PAD
    return jnp.concatenate(
        [values[start + PAD : start + pitch] for start in range(0, values.shape[0], pitch)], axis=0
    )


def rolled(values, by):
    return [values.astype(BF16)] + [
        pltpu.roll(values, (k * by) % values.shape[0], 0).astype(BF16) for k in (1, 2)
    ]


def normalized(before):
    centred = before - jnp.mean(before, axis=-1, keepdims=True)
    inv_std = lax.rsqrt(jnp.mean(centred * centred, axis=-1, keepdims=True) + 1e-05)
    return centred * inv_std, inv_std


def forward(values, weight_ref, gain, spacing):
    width = values.shape[1]
    before = jnp.zeros(values.shape, F32)
    for k, tap in enumerate(rolled(values, spacing)):
        before += jnp.dot(tap, weight_ref[k * width : (k + 1) * width, :], preferred_element_type=F32)
    normal, inv_std = normalized(before)
    output, slope = gelu_parts(normal * gain)
    return output, normal, inv_std, slope


def backward(grad_output, values, saved, weight_ref, gain, spacing, weight_grad_ref):
    normal, inv_std, slope = saved
    width = values.shape[1]
    scaled = grad_output * slope
    gain_grad = jnp.sum(scaled * normal, axis=0, keepdims=True)
    back = scaled * gain
    before = inv_std * (
        back
        - jnp.mean(back, axis=-1, keepdims=True)
        - normal * jnp.mean(back * normal, axis=-1, keepdims=True)
    )
    grad_input = jnp.zeros(values.shape, F32)
    taken = values.astype(BF16)
    for k, tap in enumerate(rolled(before, -spacing)):
        rows = slice(k * width, (k + 1) * width)
        grad_input += lax.dot_general(
            tap, weight_ref[rows, :], (((1,), (1,)), ((), ())), preferred_element_type=F32
        )
        weight_grad_ref[rows, :] += lax.dot_general(
            taken, tap, (((0,), (0,)), ((), ())), preferred_element_type=F32
        )
    return grad_input, gain_grad


def block_kernel(
    length, place_ref, got_ref, w1_ref, g1_ref, w2_ref, g2_ref, top_ref,
    out_ref, grad_ref, dw1_ref, dw2_ref, gains_ref, wide, total,
):
    items, width = out_ref.shape
    slots = got_ref.shape[0]
    step = slots // 16

    @pl.loop(0, 16)
    def _(c):
        widen(got_ref, wide, step, pl.multiple_of(c * step, 16))

    @pl.loop(0, items // 16)
    def _(g):
        at = pl.multiple_of(g * 16, 16)
        for k in range(16):
            a, b, c = [wide[pair(place_ref[t * items + at + k]), :] for t in range(3)]
            total[pl.ds(2 * at + 2 * k, 2), :] = a + b + c

    dw1_ref[...] = jnp.zeros(dw1_ref.shape, F32)
    dw2_ref[...] = jnp.zeros(dw2_ref.shape, F32)
    gains_ref[...] = jnp.zeros(gains_ref.shape, F32)
    chunk = 2 * length
    pitch = length + PAD
    row = lax.broadcasted_iota(I32, (2 * pitch, width), 0)
    real = ((row >= PAD) & (row < pitch)) | (row >= pitch + PAD)
    g1, g2 = g1_ref[...], g2_ref[...]

    @pl.loop(0, items // chunk)
    def _(c):
        at = pl.ds(pl.multiple_of(c * chunk, 16), chunk)
        embedded = jnp.concatenate(
            [total[pl.ds(2 * c * chunk + h, chunk, stride=2), :] for h in range(2)], axis=1
        )
        embedded = padded(embedded.astype(BF16).astype(F32), length)
        act_one, *saved_one = forward(embedded, w1_ref, g1, 1)
        hidden = jnp.where(real, act_one, 0.0).astype(BF16).astype(F32)
        act_two, *saved_two = forward(hidden, w2_ref, g2, 2)
        out_ref[at, :] = unpadded(embedded + act_two, length).astype(BF16)
        top = padded(top_ref[at, :].astype(F32), length)
        grad_hidden, gain_two = backward(top, hidden, saved_two, w2_ref, g2, 2, dw2_ref)
        grad_hidden = jnp.where(real, grad_hidden, 0.0)
        grad_inner, gain_one = backward(grad_hidden, embedded, saved_one, w1_ref, g1, 1, dw1_ref)
        grad_ref[at, :] = unpadded(top + grad_inner, length).astype(BF16)
        gains_ref[0:1, :] += gain_one
        gains_ref[1:2, :] += gain_two


def block_pass(place, got, length, weight_one, gain_one, weight_two, gain_two, grad_top):
    items, width = grad_top.shape
    operands = (got, weight_one, gain_one.reshape(1, -1), weight_two, gain_two.reshape(1, -1), grad_top)
    shapes = [
        ((items, width), BF16),
        ((items, width), BF16),
        (weight_one.shape, F32),
        (weight_two.shape, F32),
        ((8, width), F32),
    ]
    return pl.pallas_call(
        functools.partial(block_kernel, length),
        out_shape=[jax.ShapeDtypeStruct(*shape) for shape in shapes],
        grid_spec=pltpu.PrefetchScalarGridSpec(
            num_scalar_prefetch=1,
            grid=(1,),
            in_specs=[whole(operand.shape) for operand in operands],
            out_specs=[whole(shape) for shape, _ in shapes],
            scratch_shapes=[pltpu.VMEM((2 * got.shape[0], 128), F32), pltpu.VMEM((2 * items, 128), F32)],
        ),
        cost_estimate=pl.CostEstimate(flops=4 * 10**9, bytes_accessed=30 * 10**6, transcendentals=10**6),
        name="block_pass",
    )(place, *operands)


def collect_kernel(ways, idx_ref, got_ref, out_ref, wide, *accs):
    b = pl.program_id(0)
    block = got_ref.shape[0]
    rows = accs[0].shape[0] // 2 - 8
    unroll = 32

    @pl.when(b == 0)
    def _():
        @pl.loop(0, rows // 256)
        def _(c):
            for acc in accs:
                acc[pl.ds(pl.multiple_of(c * 512, 512), 512), :] = jnp.zeros((512, 128), F32)

    widen(got_ref, wide, block)

    @pl.loop(0, block // unroll)
    def _(g):
        at = pl.multiple_of(g * (2 * unroll), 2 * unroll)
        spots = [pair(idx_ref[b * block + g * unroll + k]) for k in range(unroll)]
        for k in range(0, unroll, ways):
            olds = [accs[j][spots[k + j], :] for j in range(ways)]
            adds = [wide[pl.ds(at + 2 * (k + j), 2), :] for j in range(ways)]
            for j in range(ways):
                accs[j][spots[k + j], :] = olds[j] + adds[j]

    @pl.when(b == pl.num_programs(0) - 1)
    def _():
        @pl.loop(0, rows // 256)
        def _(c):
            per = out_ref.shape[2] // 256
            to = pl.ds(pl.multiple_of((c % per) * 256, 256), 256)
            for half in range(2):
                at = pl.ds(c * 512 + half, 256, stride=2)
                total = accs[0][at, :]
                for acc in accs[1:]:
                    total = total + acc[at, :]
                out_ref[c // per, 128 * half : 128 * half + 128, to] = total.T.astype(BF16)


def collect(idx, got, rows, block=2432, ways=4):
    n, width = got.shape
    shape = (3, width, rows // 3)
    return pl.pallas_call(
        functools.partial(collect_kernel, ways),
        out_shape=jax.ShapeDtypeStruct(shape, BF16),
        grid_spec=pltpu.PrefetchScalarGridSpec(
            num_scalar_prefetch=1,
            grid=(n // block,),
            in_specs=[pl.BlockSpec((block, width), lambda b, i: (b, 0))],
            out_specs=whole(shape),
            scratch_shapes=[pltpu.VMEM((2 * block, 128), F32)]
            + [pltpu.VMEM((2 * (rows + 8), 128), F32)] * ways,
        ),
        cost_estimate=pl.CostEstimate(flops=10**7, bytes_accessed=60 * 10**6, transcendentals=0),
        name="collect",
    )(idx, got)


def peer_of(axis, step):
    name, size, stride = AXES[axis]
    index = lax.axis_index(name)
    mine = lax.rem(lax.div(index, stride), size)
    other = lax.rem(mine + step, size)
    return mine, other, {name: index + (other - mine) * stride}


def visit(step):
    (_, ysize, ystride), (_, zsize, zstride), (_, csize, _) = AXES[1:]
    me = lax.axis_index("table")
    y, z, c = lax.div(me, ystride), lax.rem(lax.div(me, zstride), zsize), lax.rem(me, csize)
    turn = lax.rem(step, zsize)
    half = lax.div(turn + 1, 2)
    away = jnp.where(lax.rem(turn, 2) == 1, half, zsize - half)
    y = lax.rem(y + lax.rem(lax.div(step, zsize), ysize), ysize)
    z = lax.rem(z + away, zsize)
    c = lax.rem(c + lax.div(step, zsize * ysize), csize)
    return y * ystride + z * zstride + c


def remote(src, dst, send, recv, device):
    return pltpu.make_async_remote_copy(
        src_ref=src, dst_ref=dst, send_sem=send, recv_sem=recv, device_id=device, device_id_type=MESH
    )


def exchange_kernel(scale, idx_ref, table_ref, *rest):
    summing = scale is not None
    if summing:
        w1_ref, w2_ref, gains_ref, got_ref, out_ref, wide, stage, held, own_sem, sends, recv, *more = rest
        part, r0, s0, r1, a1, xsend, xrecv, tsend, trecv, gsend, grecv, ysend, yrecv = more
    else:
        got_ref, wide, stage, held, own_sem, sends, recv = rest
    shards, cap, width = held.shape
    rows = table_ref.shape[0]
    me = lax.axis_index("table")
    group = GROUP
    total = shards - 1

    barrier = pltpu.get_barrier_semaphore()

    def hello(step, _):
        pl.semaphore_signal(barrier, inc=1, device_id={"table": visit(step)}, device_id_type=MESH)
        return 0

    lax.fori_loop(1, shards, hello, 0)
    if summing:
        for step in range(1, AXES[0][1]):
            pl.semaphore_signal(barrier, inc=1, device_id=peer_of(0, step)[2], device_id_type=MESH)

    def widened(c, _):
        at = pl.ds(pl.multiple_of(c * 64, 64), 64)
        wide[at, :] = table_ref[at, :].astype(F32)
        return 0

    lax.fori_loop(0, rows // 64, widened, 0)
    if summing:
        n, m = part.shape[1], w1_ref.shape[0]
        part[0] = w1_ref[0:n]
        part[1, 0 : m - n] = w1_ref[n:m]
        part[1, m - n : n] = w2_ref[0 : 2 * n - m]
        part[2] = w2_ref[2 * n - m : m]
        part[3, 0] = gains_ref[...]
        part[3, 1:] = jnp.zeros((n - 1,) + part.shape[2:], F32)

    def gather(step):
        dest = visit(step)
        for k in range(0, cap, 8):
            rows8 = [wide[pl.ds(idx_ref[dest * cap + k + j], 1), :] for j in range(8)]
            stage[k : k + 8, :] = jnp.concatenate(rows8, axis=0)
        held[step] = stage[...].astype(BF16)

    def post(step):
        remote(
            held.at[step],
            got_ref.at[me],
            sends.at[lax.div(step - 1, group)],
            recv,
            {"table": visit(step)},
        ).start()

    def sent(number, count):
        ref = held.at[pl.ds(0, count)]
        remote(ref, ref, sends.at[number], recv, {"table": visit(1)}).wait_send()

    gather(0)
    own = pltpu.make_async_copy(held.at[0], got_ref.at[me], own_sem)
    gather(1)
    pl.semaphore_wait(barrier, total + (AXES[0][1] - 1 if summing else 0))
    own.start()
    if summing:
        xcopies = []
        for step in range(1, AXES[0][1]):
            _, other, device = peer_of(0, step)
            xcopies.append(
                remote(part.at[other], r0.at[step - 1], xsend.at[step - 1], xrecv.at[step - 1], device)
            )
            xcopies[-1].start()
        xmine = peer_of(0, 1)[0]

    def go(step, _):
        gather(step)
        post(step - 1)
        return 0

    groups = -(-total // group)
    for number in range(groups):
        if summing and number >= 2:
            sent(number - 2, group)
        low, high = number * group + 2, min((number + 1) * group + 1, shards - 1)
        lax.fori_loop(low, high + 1, go, 0)
        if number == groups - 1:
            post(shards - 1)
        if summing and number == min(2, groups - 1):
            value = part[xmine]
            for step, copy in enumerate(xcopies):
                copy.wait_recv()
                value = value + r0[step]
            s0[...] = value

            def give(step, _):
                dest = visit(step)
                remote(s0.at[dest], r1.at[me], tsend, trecv, {"table": dest}).start()
                return 0

            r1[me] = s0[me]
            lax.fori_loop(1, shards, give, 0)
        if summing and number == min(4, groups - 1):
            many = s0.at[pl.ds(0, total)]
            remote(many, r1.at[pl.ds(0, total)], tsend, trecv, {"table": visit(1)}).wait_recv()
            a1[me] = lax.fori_loop(0, shards, lambda t, v: v + r1[t], jnp.zeros(a1.shape[1:], F32)) * scale

            def show(step, _):
                remote(a1.at[me], a1.at[me], gsend, grecv, {"table": visit(step)}).start()
                return 0

            lax.fori_loop(1, shards, show, 0)
        if summing and number == min(6, groups - 1):
            many = a1.at[pl.ds(0, total)]
            remote(many, many, gsend, grecv, {"table": visit(1)}).wait_recv()
            ycopies = []
            for step in range(1, AXES[0][1]):
                copy = remote(a1, out_ref.at[xmine], ysend.at[step - 1], yrecv.at[step - 1], peer_of(0, step)[2])
                copy.start()
                ycopies.append(copy)
            out_ref[xmine] = a1[...]
    for number in range(groups):
        if not summing or number >= groups - 2:
            sent(number, min(group, total - number * group))
    own.wait()
    ref = held.at[pl.ds(0, total)]
    remote(ref, got_ref.at[pl.ds(0, total)], sends.at[0], recv, {"table": visit(1)}).wait_recv()
    if summing:
        for copy in xcopies:
            copy.wait_send()
        many = a1.at[pl.ds(0, total)]
        remote(many, many, tsend, trecv, {"table": visit(1)}).wait_send()
        remote(many, many, gsend, grecv, {"table": visit(1)}).wait_send()
        for copy in ycopies:
            copy.wait()


def exchange(idx, table, shards, collective_id, name, sums=None):
    (rows, width), cap = table.shape, idx.shape[0] // shards
    any_space, vmem = pl.BlockSpec(memory_space=pl.ANY), pl.BlockSpec(memory_space=pltpu.VMEM)
    out_shape = [jax.ShapeDtypeStruct((shards, cap, width), BF16)]
    out_specs = [any_space]
    scratch = [
        pltpu.VMEM((rows, width), F32),
        pltpu.VMEM((cap, width), F32),
        pltpu.VMEM((shards, cap, width), BF16),
        pltpu.SemaphoreType.DMA,
        pltpu.SemaphoreType.DMA((-(-(shards - 1) // GROUP),)),
        pltpu.SemaphoreType.DMA,
    ]
    operands, scale = [], None
    if sums is not None:
        *operands, scale = sums
        xsize = AXES[0][1]
        tile = operands[0].shape[1:]
        out_shape.append(jax.ShapeDtypeStruct((xsize, shards) + tile, F32))
        out_specs.append(vmem)
        block = (shards,) + tile
        scratch += [
            pltpu.VMEM((xsize,) + block, F32),
            pltpu.VMEM((xsize - 1,) + block, F32),
            pltpu.VMEM(block, F32),
            pltpu.VMEM(block, F32),
            pltpu.VMEM(block, F32),
        ]
        several, one = pltpu.SemaphoreType.DMA((xsize - 1,)), pltpu.SemaphoreType.DMA
        scratch += [several, several, one, one, one, one, several, several]
    return pl.pallas_call(
        functools.partial(exchange_kernel, scale),
        out_shape=out_shape,
        in_specs=[pl.BlockSpec(memory_space=pltpu.SMEM)] + [vmem] * (1 + len(operands)),
        out_specs=out_specs,
        scratch_shapes=scratch,
        compiler_params=pltpu.CompilerParams(collective_id=collective_id, has_side_effects=True),
        cost_estimate=pl.CostEstimate(flops=10**7, bytes_accessed=10**8, transcendentals=0),
        name=name,
    )(idx, table, *operands)


def greet(steps):
    barrier = pltpu.get_barrier_semaphore()
    for axis, step in steps:
        pl.semaphore_signal(barrier, inc=1, device_id=peer_of(axis, step)[2], device_id_type=MESH)
    pl.semaphore_wait(barrier, len(steps))


def group_sum_kernel(dense_ref, out_ref, own, land, local, send, recv):
    tables, quarter, _ = out_ref.shape
    greet([(0, step) for step in range(1, 4)])
    copies = []
    for t in range(tables):
        for step in range(1, 4):
            mine, other, device = peer_of(0, step)
            copy = pltpu.make_async_remote_copy(
                src_ref=dense_ref.at[t, pl.ds(pl.multiple_of(other * quarter, quarter), quarter)],
                dst_ref=land.at[t, step - 1],
                send_sem=send.at[3 * t + step - 1],
                recv_sem=recv.at[3 * t + step - 1],
                device_id=device,
                device_id_type=MESH,
            )
            copy.start()
            copies.append(copy)
    mine = peer_of(0, 1)[0]
    mine_at = pl.ds(pl.multiple_of(mine * quarter, quarter), quarter)
    kept = [pltpu.make_async_copy(dense_ref.at[t, mine_at], own.at[t], local.at[t]) for t in range(tables)]
    for copy in kept:
        copy.start()
    for t in range(tables):
        kept[t].wait()
        for step in range(3):
            copies[3 * t + step].wait_recv()
        total = own[t].astype(F32)
        for step in range(3):
            total = total + land[t, step].astype(F32)
        out_ref[t] = total
    for copy in copies:
        copy.wait_send()


def group_sum(dense):
    tables, width, rows = dense.shape
    quarter = width // 4
    return pl.pallas_call(
        group_sum_kernel,
        out_shape=jax.ShapeDtypeStruct((tables, quarter, rows), F32),
        in_specs=[pl.BlockSpec(memory_space=pl.ANY)],
        out_specs=pl.BlockSpec(memory_space=pltpu.VMEM),
        scratch_shapes=[
            pltpu.VMEM((tables, quarter, rows), BF16),
            pltpu.VMEM((tables, 3, quarter, rows), BF16),
            pltpu.SemaphoreType.DMA((tables,)),
            pltpu.SemaphoreType.DMA((3 * tables,)),
            pltpu.SemaphoreType.DMA((3 * tables,)),
        ],
        compiler_params=pltpu.CompilerParams(collective_id=2, has_side_effects=True),
        cost_estimate=pl.CostEstimate(flops=10**6, bytes_accessed=60 * 10**6, transcendentals=0),
        name="group_sum",
    )(dense)


def on_device(shard_of, offsets, table, weight_one, gain_one, weight_two, gain_two, grad_out):
    sessions, length, _ = shard_of.shape
    width = table.shape[2]
    rows_dev = table.shape[1]
    rows = 3 * rows_dev
    item_count = sessions * length
    shards = lax.axis_size("table")
    groups = lax.axis_size("dp")
    slot_count = 8 * ((6 * item_count + 8 * shards - 1) // (8 * shards))
    place, requests, items = make_index(
        jnp.transpose(shard_of, (2, 0, 1)), jnp.transpose(offsets, (2, 0, 1)), shards, slot_count, rows_dev
    )
    asked = lax.all_to_all(requests, "table", split_axis=0, concat_axis=0, tiled=True).reshape(-1)
    found = jnp.maximum(asked - 1, 0)
    spots = jnp.where(asked > 0, asked - 1, rows)
    (got,) = exchange(found, table.reshape(rows, width), shards, 0, "rows_out")
    scale = 1.0 / math.sqrt(item_count * groups * shards)
    block_out, grad_embed, first_weights, second_weights, gains = block_pass(
        place.reshape(-1),
        got.reshape(-1, width),
        length,
        weight_one,
        gain_one,
        weight_two,
        gain_two,
        grad_out.reshape(item_count, width),
    )
    tiles = (-1, 8, width)
    arrived, totals = exchange(
        items.reshape(-1),
        grad_embed,
        shards,
        1,
        "grads_out",
        (first_weights.reshape(tiles), second_weights.reshape(tiles), gains, scale),
    )
    totals = totals.reshape(-1, width)
    dense = collect(spots, arrived.reshape(-1, width), rows)
    table_grad = jnp.transpose(group_sum(dense), (0, 2, 1))
    block_out = block_out.reshape(sessions, length, width)
    return block_out, totals[:768], totals[768:1536], totals[1536], totals[1537], table_grad


def solution(mesh):
    placed = (
        P(("dp", "table"), None, None),
        P(("dp", "table"), None, None),
        P(None, "table", None),
        P(),
        P(),
        P(),
        P(),
        P(("dp", "table"), None, None),
    )
    return jax.shard_map(
        on_device,
        mesh=mesh,
        in_specs=placed,
        out_specs=(P(("dp", "table"), None, None), P(), P(), P(), P(), P(None, "table", "dp")),
        check_vma=False,
    )
```

profile of v0, /device:TPU:2, one launch (start us, length us, event | category | flops | bytes accessed | tf_op | source)
XLA Modules:
  0.0 397.7 jit_solution(4660540783141155123)
XLA Ops:
  0.6 8.1 %index.1 = (s32[3,8,200]{2,1,0:T(8,128)}, s32[64,152]{1,0:T(8,128)}, s32[64,152]{1,0:T(8,128)}) custom-call(s32[3,8,200]{2,1,0:T(8,128)} %bitcast.28, s32[3,8,200]{2,1,0:T(8,128)} %bitcast.29), custom_call_target="tpu_custom_call" | custom-call | flops 1000000000 | bytes 1000000 | tf_op jit(solution)/shard_map/index/pallas_call | solution.py:66
  8.8 1.5 copy.14
  10.3 12.3 %all-to-all-start = ((s32[64,1,152]{2,1,0:T(1,128)}), s32[64,1,152]{2,1,0:T(1,128)S(1)}, u32[]{:S(2)}, u32[]{:S(2)}) async-start(s32[64,1,152]{2,1,0:T(1,128)} %copy.14), calls=%async_computation | async-start | bytes 131072 | tf_op jit(solution)/shard_map/all_to_all | solution.py:563
  22.6 1.5 reshape.60.place_ref
  24.0 1.6 reshape.67.idx_ref
  25.6 6.5 %all-to-all-done = s32[64,1,152]{2,1,0:T(1,128)S(1)} async-done(((s32[64,1,152]{2,1,0:T(1,128)}), s32[64,1,152]{2,1,0:T(1,128)S(1)}, u32[]{:S(2)}, u32[]{:S(2)}) %all-to-all-start) | async-done | bytes 38944 | tf_op jit(solution)/shard_map/all_to_all | solution.py:563
  32.1 0.4 fusion
  32.5 0.7 max.6.idx_ref
  33.2 119.6 %rows_out.1 = bf16[64,152,256]{2,1,0:T(8,128)(2,1)} custom-call(s32[9728]{0:T(1024)} %max.6.idx_ref, bf16[6144,256]{1,0:T(8,128)(2,1)} %bitcast.19), custom_call_target="tpu_custom_call" | custom-call | flops 10000000 | bytes 100000000 | tf_op jit(solution)/shard_map/rows_out/pallas_call | solution.py:477
  152.8 22.6 %block_pass.1 = (bf16[1600,256]{1,0:T(8,128)(2,1)}, bf16[1600,256]{1,0:T(8,128)(2,1)}, f32[768,256]{1,0:T(8,128)}, f32[768,256]{1,0:T(8,128)}, f32[8,256]{1,0:T(8,128)}) custom-call(s32[4800]{0:T(1024)} %reshape.60.place_ref, bf16[9728,256]{1,0:T(8,128)(2,1)} %bitcast.18, bf16[768,256]{1,0:T(8,128)(2,1)} %w1_ref.1, f32[1,256]{1,0:T(1,128)} %bitcast.30, ...), custom_call_target="tpu_custom_call" | custom-call | flops 4000000000 | bytes 30000000 | tf_op jit(solution)/shard_map/block_pass/pallas_call | solution.py:211
  175.4 151.0 %grads_out.1 = (bf16[64,152,256]{2,1,0:T(8,128)(2,1)}, f32[4,64,8,256]{3,2,1,0:T(8,128)}) custom-call(s32[9728]{0:T(1024)} %reshape.67.idx_ref, bf16[1600,256]{1,0:T(8,128)(2,1)} %get-tuple-element.20.table_ref, f32[96,8,256]{2,1,0:T(8,128)} %bitcast.22, f32[96,8,256]{2,1,0:T(8,128)} %bitcast.23, f32[8,256]{1,0:T(8,128)} %get-tuple-element.23.rest_2_), custom_call_target="tpu_custom_call" | custom-call | flops 10000000 | bytes 100000000 | tf_op jit(solution)/shard_map/grads_out/pallas_call | solution.py:477
  326.4 2.6 fusion.2
  329.0 1.3 fusion.1
  330.4 0.7 select_n.7.idx_ref
  331.1 25.7 %collect.1.dense_ref = bf16[3,256,2048]{2,1,0:T(8,128)(2,1)} custom-call(s32[9728]{0:T(1024)} %select_n.7.idx_ref, bf16[9728,256]{1,0:T(8,128)(2,1)} %bitcast.17), custom_call_target="tpu_custom_call" | custom-call | flops 10000000 | bytes 60000000 | tf_op jit(solution)/shard_map/collect/pallas_call | solution.py:268
  356.8 38.2 %group_sum.1 = f32[3,64,2048]{2,1,0:T(8,128)} custom-call(bf16[3,256,2048]{2,1,0:T(8,128)(2,1)} %collect.1.dense_ref), custom_call_target="tpu_custom_call" | custom-call | flops 1000000 | bytes 60000000 | tf_op jit(solution)/shard_map/group_sum/pallas_call | solution.py:533
  395.0 2.7 copy.16
Async XLA Ops:
  10.3 21.8 %all-to-all-start = ((s32[64,1,152]{2,1,0:T(1,128)}), s32[64,1,152]{2,1,0:T(1,128)S(1)}, u32[]{:S(2)}, u32[]{:S(2)}) async-start(s32[64,1,152]{2,1,0:T(1,128)} %copy.14), calls=%async_computation | async-start | bytes 131072 | tf_op jit(solution)/shard_map/all_to_all | solution.py:563
where the time goes:
time: 402 us; the launch traced here: 398 us
  Pallas kernels  365 us (91%)
  local copies, waits for them, and re-layouts  12.6 us (3%)
  starting transfers between devices  12.3 us (3%)
  waiting for transfers between devices  6.53 us (2%)
    pallas_call x2, Pallas kernels, exchange(): pl.pallas_call(functools.partial(exchange_kernel, scale), out_shape=out_s...  271 us
    pallas_call x1, Pallas kernels, group_sum(): pl.pallas_call(group_sum_kernel, out_shape=jax.ShapeDtypeStruct((tables,...  38.2 us
    pallas_call x1, Pallas kernels, collect(): pl.pallas_call(functools.partial(collect_kernel, ways), out_shape=jax.Sha...  25.7 us
    pallas_call x1, Pallas kernels, block_pass(): pl.pallas_call(functools.partial(block_kernel, length), out_shape=[jax.Sh...  22.6 us
    all_to_all x1, starting transfers between devices, on_device(): lax.all_to_all(requests, 'table', split_axis=0, concat_axis=0, tiled=True)  12.3 us
    pallas_call x1, Pallas kernels, make_index(): pl.pallas_call(functools.partial(index_kernel, shards, cap, rows_dev), ou...  8.13 us
  transfers between devices with their start and end apart: 1, of which 1 were waited for; matrix products, arithmetic and copies ran while one was open for 1% of the time, Pallas kernels for 0%

commit v1 on v0

--- a/solution.py
+++ b/solution.py
@@ -12,6 +12,8 @@
 MESH = pl.DeviceIdType.MESH
 GELU_C = 0.7978845608028654
 GELU_K = 0.044715
+PITCH = 256
+EDGE = 8
 GROUP = 8
 AXES = (("dp", 4, 1), ("table", 4, 16), ("table", 8, 2), ("table", 2, 1))
 
@@ -26,8 +28,17 @@
     return (output, slope)
 
 
-def index_kernel(shards, cap, rows_dev, sh_ref, off_ref, place_ref, req_ref, item_ref):
+def index_kernel(cap, rows_dev, sh_ref, off_ref, place_ref, asked_ref, item_ref, req_ref, send, recv):
     tables, sessions, length = sh_ref.shape
+    shards = asked_ref.shape[0]
+    me = lax.axis_index("table")
+    barrier = pltpu.get_barrier_semaphore()
+
+    def hello(step, _):
+        pl.semaphore_signal(barrier, inc=1, device_id={"table": visit(step)}, device_id_type=MESH)
+        return 0
+
+    lax.fori_loop(1, shards, hello, 0)
     tri = (
         lax.broadcasted_iota(I32, (length, length), 0) < lax.broadcasted_iota(I32, (length, length), 1)
     ).astype(BF16)
@@ -40,15 +51,17 @@
     for t in range(tables):
         for s in range(sessions):
             sh = sh_ref[t, s : s + 1, :]
-            code = off_ref[t, s : s + 1, :] + (t * rows_dev + 1)
-            item = lane + s * length
+            code = off_ref[t, s : s + 1, :] + (t * rows_dev + EDGE)
+            item = lane + (s * length + EDGE)
             hit = shard_id == sh
             hot = jnp.where(hit, 1.0, 0.0)
             hot16 = hot.astype(BF16)
             prefix = jnp.dot(hot16, tri, preferred_element_type=F32) + base
             rank = jnp.sum(jnp.where(hit, prefix, 0.0), axis=0, keepdims=True).astype(I32)
             base = base + jnp.sum(hot, axis=1, keepdims=True)
-            place_ref[t, s : s + 1, :] = sh * cap + rank
+            place = sh * cap + rank
+            place_ref[t * sessions + s, 0:1, :] = place[:, :128]
+            place_ref[t * sessions + s, 1:2, 0 : length - 128] = place[:, 128:]
             here = slot_id == rank
             for n, digit in enumerate((code // 256, code % 256, item // 256, item % 256)):
                 listed[n] += lax.dot_general(
@@ -57,15 +70,35 @@
                     dims,
                     preferred_element_type=F32,
                 )
-    req_ref[...] = (listed[0] * 256.0 + listed[1]).astype(I32)
-    item_ref[...] = (listed[2] * 256.0 + listed[3]).astype(I32)
+    for ref, high, low in ((req_ref, listed[0], listed[1]), (item_ref, listed[2], listed[3])):
+        codes = (high * 256.0 + low).astype(I32)
+        ref[...] = jnp.zeros(ref.shape, I32)
+        ref[:, 0, :] = codes[:, :128]
+        ref[:, 1, 0 : cap - 128] = codes[:, 128:]
+    pl.semaphore_wait(barrier, shards - 1)
+
+    def ask(step, _):
+        dest = visit(step)
+        remote(req_ref.at[dest], asked_ref.at[me], send, recv, {"table": dest}).start()
+        return 0
+
+    lax.fori_loop(1, shards, ask, 0)
+    asked_ref[me] = req_ref[me]
+    many = pl.ds(0, shards - 1)
+    remote(req_ref.at[many], asked_ref.at[many], send, recv, {"table": visit(1)}).wait()
 
 
 def make_index(sh, off, shards, cap, rows_dev):
-    block = jax.ShapeDtypeStruct((shards, cap), I32)
+    tables, sessions, _ = sh.shape
+    block = jax.ShapeDtypeStruct((shards, 2, 128), I32)
+    vmem = pl.BlockSpec(memory_space=pltpu.VMEM)
     return pl.pallas_call(
-        functools.partial(index_kernel, shards, cap, rows_dev),
-        out_shape=(jax.ShapeDtypeStruct(sh.shape, I32), block, block),
+        functools.partial(index_kernel, cap, rows_dev),
+        out_shape=(jax.ShapeDtypeStruct((tables * sessions, 2, 128), I32), block, block),
+        in_specs=[vmem] * 2,
+        out_specs=[vmem] * 3,
+        scratch_shapes=[pltpu.VMEM((shards, 2, 128), I32), pltpu.SemaphoreType.DMA, pltpu.SemaphoreType.DMA],
+        compiler_params=pltpu.CompilerParams(collective_id=3, has_side_effects=True),
         cost_estimate=pl.CostEstimate(flops=10**9, bytes_accessed=10**6, transcendentals=0),
         name="index",
     )(sh, off)
@@ -162,12 +195,16 @@
     def _(c):
         widen(got_ref, wide, step, pl.multiple_of(c * step, 16))
 
-    @pl.loop(0, items // 16)
+    sessions = items // length
+
+    @pl.loop(0, items // 40)
     def _(g):
-        at = pl.multiple_of(g * 16, 16)
-        for k in range(16):
-            a, b, c = [wide[pair(place_ref[t * items + at + k]), :] for t in range(3)]
-            total[pl.ds(2 * at + 2 * k, 2), :] = a + b + c
+        session = g // (length // 40)
+        at = session * PITCH + (g - session * (length // 40)) * 40
+        to = pl.multiple_of(g * 80, 16)
+        for k in range(40):
+            a, b, c = [wide[pair(place_ref[t * sessions * PITCH + at + k]), :] for t in range(3)]
+            total[pl.ds(to + 2 * k, 2), :] = a + b + c
 
     dw1_ref[...] = jnp.zeros(dw1_ref.shape, F32)
     dw2_ref[...] = jnp.zeros(dw2_ref.shape, F32)
@@ -223,30 +260,30 @@
     )(place, *operands)
 
 
-def collect_kernel(ways, idx_ref, got_ref, out_ref, wide, *accs):
+def collect_kernel(ways, cap, idx_ref, got_ref, out_ref, wide, *accs):
     b = pl.program_id(0)
     block = got_ref.shape[0]
-    rows = accs[0].shape[0] // 2 - 8
-    unroll = 32
+    rows = accs[0].shape[0] // 2 - EDGE
 
     @pl.when(b == 0)
     def _():
         @pl.loop(0, rows // 256)
         def _(c):
             for acc in accs:
-                acc[pl.ds(pl.multiple_of(c * 512, 512), 512), :] = jnp.zeros((512, 128), F32)
+                acc[pl.ds(pl.multiple_of(2 * EDGE + c * 512, 16), 512), :] = jnp.zeros((512, 128), F32)
 
     widen(got_ref, wide, block)
 
-    @pl.loop(0, block // unroll)
+    @pl.loop(0, block // cap)
     def _(g):
-        at = pl.multiple_of(g * (2 * unroll), 2 * unroll)
-        spots = [pair(idx_ref[b * block + g * unroll + k]) for k in range(unroll)]
-        for k in range(0, unroll, ways):
-            olds = [accs[j][spots[k + j], :] for j in range(ways)]
+        at = pl.multiple_of(g * (2 * cap), 16)
+        base = (b * (block // cap) + g) * PITCH
+        for k in range(0, cap, ways):
+            spots = [pair(idx_ref[base + k + j]) for j in range(ways)]
+            olds = [accs[j][spots[j], :] for j in range(ways)]
             adds = [wide[pl.ds(at + 2 * (k + j), 2), :] for j in range(ways)]
             for j in range(ways):
-                accs[j][spots[k + j], :] = olds[j] + adds[j]
+                accs[j][spots[j], :] = olds[j] + adds[j]
 
     @pl.when(b == pl.num_programs(0) - 1)
     def _():
@@ -255,18 +292,18 @@
             per = out_ref.shape[2] // 256
             to = pl.ds(pl.multiple_of((c % per) * 256, 256), 256)
             for half in range(2):
-                at = pl.ds(c * 512 + half, 256, stride=2)
+                at = pl.ds(2 * EDGE + c * 512 + half, 256, stride=2)
                 total = accs[0][at, :]
                 for acc in accs[1:]:
                     total = total + acc[at, :]
                 out_ref[c // per, 128 * half : 128 * half + 128, to] = total.T.astype(BF16)
 
 
-def collect(idx, got, rows, block=2432, ways=4):
+def collect(idx, got, rows, cap, block=2432, ways=4):
     n, width = got.shape
     shape = (3, width, rows // 3)
     return pl.pallas_call(
-        functools.partial(collect_kernel, ways),
+        functools.partial(collect_kernel, ways, cap),
         out_shape=jax.ShapeDtypeStruct(shape, BF16),
         grid_spec=pltpu.PrefetchScalarGridSpec(
             num_scalar_prefetch=1,
@@ -274,7 +311,7 @@
             in_specs=[pl.BlockSpec((block, width), lambda b, i: (b, 0))],
             out_specs=whole(shape),
             scratch_shapes=[pltpu.VMEM((2 * block, 128), F32)]
-            + [pltpu.VMEM((2 * (rows + 8), 128), F32)] * ways,
+            + [pltpu.VMEM((2 * (rows + EDGE), 128), F32)] * ways,
         ),
         cost_estimate=pl.CostEstimate(flops=10**7, bytes_accessed=60 * 10**6, transcendentals=0),
         name="collect",
@@ -312,7 +349,7 @@
     summing = scale is not None
     if summing:
         w1_ref, w2_ref, gains_ref, got_ref, out_ref, wide, stage, held, own_sem, sends, recv, *more = rest
-        part, r0, s0, r1, a1, xsend, xrecv, tsend, trecv, gsend, grecv, ysend, yrecv = more
+        part, r0, s0, r1, s1, r2, a2, a1, *sems = more
     else:
         got_ref, wide, stage, held, own_sem, sends, recv = rest
     shards, cap, width = held.shape
@@ -334,23 +371,55 @@
 
     def widened(c, _):
         at = pl.ds(pl.multiple_of(c * 64, 64), 64)
-        wide[at, :] = table_ref[at, :].astype(F32)
+        wide[pl.ds(pl.multiple_of(EDGE + c * 64, EDGE), 64), :] = table_ref[at, :].astype(F32)
         return 0
+
+    wide[0:EDGE, :] = jnp.zeros((EDGE, width), F32)
 
     lax.fori_loop(0, rows // 64, widened, 0)
     if summing:
-        n, m = part.shape[1], w1_ref.shape[0]
-        part[0] = w1_ref[0:n]
-        part[1, 0 : m - n] = w1_ref[n:m]
-        part[1, m - n : n] = w2_ref[0 : 2 * n - m]
-        part[2] = w2_ref[2 * n - m : m]
-        part[3, 0] = gains_ref[...]
-        part[3, 1:] = jnp.zeros((n - 1,) + part.shape[2:], F32)
+        parts = [(w1_ref, w1_ref.shape[0]), (w2_ref, w2_ref.shape[0]), (gains_ref, 1)]
+        ysize, zcsize = part.shape[1:3]
+        block = 0
+        for ref, count in parts:
+            done = 0
+            while done < count:
+                many = min(count - done, zcsize - block % zcsize)
+                first = block % zcsize
+                row = ref[...][None] if ref is gains_ref else ref[done : done + many]
+                part[block // (ysize * zcsize), block // zcsize % ysize, first : first + many] = row
+                done, block = done + many, block + many
+        while block < part.shape[0] * ysize * zcsize:
+            many = zcsize - block % zcsize
+            empty = jnp.zeros((many,) + part.shape[3:], F32)
+            part[block // (ysize * zcsize), block // zcsize % ysize, block % zcsize :] = empty
+            block += many
+        ymine, zcmine = lax.div(me, zcsize), lax.rem(me, zcsize)
+        xmine = peer_of(0, 1)[0]
+        xpeers = [peer_of(0, step)[1:] for step in range(1, AXES[0][1])]
+        ypeers = [lax.rem(ymine + step, ysize) for step in range(1, ysize)]
+        ypeers = [(other, {"table": other * zcsize + zcmine}) for other in ypeers]
+        zcpeers = [lax.rem(zcmine + step, zcsize) for step in range(1, zcsize)]
+        zcpeers = [(other, {"table": ymine * zcsize + other}) for other in zcpeers]
+
+        def fan(stage, peers, src, dst):
+            send_sem, recv_sem = sems[2 * stage : 2 * stage + 2]
+            copies = [
+                remote(src(other), dst(n), send_sem.at[n], recv_sem.at[n], device)
+                for n, (other, device) in enumerate(peers)
+            ]
+            for copy in copies:
+                copy.start()
+            return copies
+
+        def landed(copies):
+            for copy in copies:
+                copy.wait_recv()
 
     def gather(step):
         dest = visit(step)
         for k in range(0, cap, 8):
-            rows8 = [wide[pl.ds(idx_ref[dest * cap + k + j], 1), :] for j in range(8)]
+            rows8 = [wide[pl.ds(idx_ref[dest * PITCH + k + j], 1), :] for j in range(8)]
             stage[k : k + 8, :] = jnp.concatenate(rows8, axis=0)
         held[step] = stage[...].astype(BF16)
 
@@ -373,14 +442,7 @@
     pl.semaphore_wait(barrier, total + (AXES[0][1] - 1 if summing else 0))
     own.start()
     if summing:
-        xcopies = []
-        for step in range(1, AXES[0][1]):
-            _, other, device = peer_of(0, step)
-            xcopies.append(
-                remote(part.at[other], r0.at[step - 1], xsend.at[step - 1], xrecv.at[step - 1], device)
-            )
-            xcopies[-1].start()
-        xmine = peer_of(0, 1)[0]
+        flights = [fan(0, xpeers, lambda other: part.at[other], lambda n: r0.at[n])]
 
     def go(step, _):
         gather(step)
@@ -395,39 +457,26 @@
         lax.fori_loop(low, high + 1, go, 0)
         if number == groups - 1:
             post(shards - 1)
-        if summing and number == min(2, groups - 1):
-            value = part[xmine]
-            for step, copy in enumerate(xcopies):
-                copy.wait_recv()
-                value = value + r0[step]
-            s0[...] = value
-
-            def give(step, _):
-                dest = visit(step)
-                remote(s0.at[dest], r1.at[me], tsend, trecv, {"table": dest}).start()
-                return 0
-
-            r1[me] = s0[me]
-            lax.fori_loop(1, shards, give, 0)
-        if summing and number == min(4, groups - 1):
-            many = s0.at[pl.ds(0, total)]
-            remote(many, r1.at[pl.ds(0, total)], tsend, trecv, {"table": visit(1)}).wait_recv()
-            a1[me] = lax.fori_loop(0, shards, lambda t, v: v + r1[t], jnp.zeros(a1.shape[1:], F32)) * scale
-
-            def show(step, _):
-                remote(a1.at[me], a1.at[me], gsend, grecv, {"table": visit(step)}).start()
-                return 0
-
-            lax.fori_loop(1, shards, show, 0)
-        if summing and number == min(6, groups - 1):
-            many = a1.at[pl.ds(0, total)]
-            remote(many, many, gsend, grecv, {"table": visit(1)}).wait_recv()
-            ycopies = []
-            for step in range(1, AXES[0][1]):
-                copy = remote(a1, out_ref.at[xmine], ysend.at[step - 1], yrecv.at[step - 1], peer_of(0, step)[2])
-                copy.start()
-                ycopies.append(copy)
-            out_ref[xmine] = a1[...]
+        if summing and number >= 1:
+            for stage in range(number, number + 1) if number < groups - 1 else range(number, 6):
+                if stage > 5:
+                    continue
+                landed(flights[-1])
+                if stage == 1:
+                    s0[...] = sum([r0[n] for n in range(len(xpeers))], part[xmine])
+                    flights.append(fan(1, ypeers, lambda other: s0.at[other], lambda n: r1.at[n]))
+                elif stage == 2:
+                    s1[...] = sum([r1[n] for n in range(len(ypeers))], s0[ymine])
+                    flights.append(fan(2, zcpeers, lambda other: s1.at[other], lambda n: r2.at[n]))
+                elif stage == 3:
+                    a2[zcmine] = sum([r2[n] for n in range(len(zcpeers))], s1[zcmine]) * scale
+                    flights.append(fan(3, zcpeers, lambda _: a2.at[zcmine], lambda _: a2.at[zcmine]))
+                elif stage == 4:
+                    flights.append(fan(4, ypeers, lambda _: a2, lambda _: a1.at[ymine]))
+                    a1[ymine] = a2[...]
+                elif stage == 5:
+                    flights.append(fan(5, xpeers, lambda _: a1, lambda _: out_ref.at[xmine]))
+                    out_ref[xmine] = a1[...]
     for number in range(groups):
         if not summing or number >= groups - 2:
             sent(number, min(group, total - number * group))
@@ -435,22 +484,19 @@
     ref = held.at[pl.ds(0, total)]
     remote(ref, got_ref.at[pl.ds(0, total)], sends.at[0], recv, {"table": visit(1)}).wait_recv()
     if summing:
-        for copy in xcopies:
-            copy.wait_send()
-        many = a1.at[pl.ds(0, total)]
-        remote(many, many, tsend, trecv, {"table": visit(1)}).wait_send()
-        remote(many, many, gsend, grecv, {"table": visit(1)}).wait_send()
-        for copy in ycopies:
-            copy.wait()
-
-
-def exchange(idx, table, shards, collective_id, name, sums=None):
-    (rows, width), cap = table.shape, idx.shape[0] // shards
+        landed(flights[-1])
+        for copies in flights:
+            for copy in copies:
+                copy.wait_send()
+
+
+def exchange(idx, table, shards, cap, collective_id, name, sums=None):
+    rows, width = table.shape
     any_space, vmem = pl.BlockSpec(memory_space=pl.ANY), pl.BlockSpec(memory_space=pltpu.VMEM)
     out_shape = [jax.ShapeDtypeStruct((shards, cap, width), BF16)]
     out_specs = [any_space]
     scratch = [
-        pltpu.VMEM((rows, width), F32),
+        pltpu.VMEM((rows + EDGE, width), F32),
         pltpu.VMEM((cap, width), F32),
         pltpu.VMEM((shards, cap, width), BF16),
         pltpu.SemaphoreType.DMA,
@@ -460,20 +506,16 @@
     operands, scale = [], None
     if sums is not None:
         *operands, scale = sums
-        xsize = AXES[0][1]
+        xsize, ysize, zcsize = AXES[0][1], AXES[1][1], AXES[1][2]
         tile = operands[0].shape[1:]
-        out_shape.append(jax.ShapeDtypeStruct((xsize, shards) + tile, F32))
+        line, plane = (zcsize,) + tile, (ysize, zcsize) + tile
+        out_shape.append(jax.ShapeDtypeStruct((xsize,) + plane, F32))
         out_specs.append(vmem)
-        block = (shards,) + tile
-        scratch += [
-            pltpu.VMEM((xsize,) + block, F32),
-            pltpu.VMEM((xsize - 1,) + block, F32),
-            pltpu.VMEM(block, F32),
-            pltpu.VMEM(block, F32),
-            pltpu.VMEM(block, F32),
-        ]
-        several, one = pltpu.SemaphoreType.DMA((xsize - 1,)), pltpu.SemaphoreType.DMA
-        scratch += [several, several, one, one, one, one, several, several]
+        shapes = [(xsize,) + plane, (xsize - 1,) + plane, plane, (ysize - 1,) + line, line]
+        shapes += [(zcsize - 1,) + tile, line, plane]
+        scratch += [pltpu.VMEM(shape, F32) for shape in shapes]
+        for size in (xsize, ysize, zcsize, zcsize, ysize, xsize):
+            scratch += [pltpu.SemaphoreType.DMA((size - 1,))] * 2
     return pl.pallas_call(
         functools.partial(exchange_kernel, scale),
         out_shape=out_shape,
@@ -493,38 +535,53 @@
     pl.semaphore_wait(barrier, len(steps))
 
 
-def group_sum_kernel(dense_ref, out_ref, own, land, local, send, recv):
+def group_sum_kernel(dense_ref, out_ref, far, mixed, near, sems):
     tables, quarter, _ = out_ref.shape
+    half = quarter // 2
     greet([(0, step) for step in range(1, 4)])
-    copies = []
+    mine, after, right = peer_of(0, 1)
+    _, across, _ = peer_of(0, 2)
+    _, before, left = peer_of(0, 3)
+    ways = ((right, after, 0), (left, before, half))
+
+    def share(t, owner, start):
+        return dense_ref.at[t, pl.ds(pl.multiple_of(owner * quarter + start, half), half)]
+
+    def hop(kind, t, way, src, dst):
+        n = (kind * tables + t) * 2 + way
+        copy = remote(src, dst, sems.at[0, n], sems.at[1, n], ways[way][0])
+        copy.start()
+        return copy
+
+    firsts = [
+        [hop(0, t, way, share(t, across, start), far.at[t, way]) for way, (_, _, start) in enumerate(ways)]
+        for t in range(tables)
+    ]
+    others = [
+        [
+            hop(1, t, way, share(t, owner, half - start), near.at[t, way, pl.ds(half - start, half)])
+            for way, (_, owner, start) in enumerate(ways)
+        ]
+        for t in range(tables)
+    ]
+    lasts = []
     for t in range(tables):
-        for step in range(1, 4):
-            mine, other, device = peer_of(0, step)
-            copy = pltpu.make_async_remote_copy(
-                src_ref=dense_ref.at[t, pl.ds(pl.multiple_of(other * quarter, quarter), quarter)],
-                dst_ref=land.at[t, step - 1],
-                send_sem=send.at[3 * t + step - 1],
-                recv_sem=recv.at[3 * t + step - 1],
-                device_id=device,
-                device_id_type=MESH,
-            )
-            copy.start()
-            copies.append(copy)
-    mine = peer_of(0, 1)[0]
-    mine_at = pl.ds(pl.multiple_of(mine * quarter, quarter), quarter)
-    kept = [pltpu.make_async_copy(dense_ref.at[t, mine_at], own.at[t], local.at[t]) for t in range(tables)]
-    for copy in kept:
-        copy.start()
+        for way, (_, owner, start) in enumerate(ways):
+            firsts[t][way].wait_recv()
+            kept = dense_ref[t, pl.ds(pl.multiple_of(owner * quarter + start, half), half), :]
+            mixed[t, way] = (far[t, way].astype(F32) + kept.astype(F32)).astype(BF16)
+        lasts.append(
+            [hop(2, t, way, mixed.at[t, way], near.at[t, way, pl.ds(start, half)]) for way, (_, _, start) in enumerate(ways)]
+        )
     for t in range(tables):
-        kept[t].wait()
-        for step in range(3):
-            copies[3 * t + step].wait_recv()
-        total = own[t].astype(F32)
-        for step in range(3):
-            total = total + land[t, step].astype(F32)
-        out_ref[t] = total
-    for copy in copies:
-        copy.wait_send()
+        for way in range(2):
+            others[t][way].wait_recv()
+            lasts[t][way].wait_recv()
+        kept = dense_ref[t, pl.ds(pl.multiple_of(mine * quarter, quarter), quarter), :]
+        out_ref[t] = kept.astype(F32) + near[t, 0].astype(F32) + near[t, 1].astype(F32)
+    for copies in firsts + others + lasts:
+        for copy in copies:
+            copy.wait_send()
 
 
 def group_sum(dense):
@@ -533,14 +590,13 @@
     return pl.pallas_call(
         group_sum_kernel,
         out_shape=jax.ShapeDtypeStruct((tables, quarter, rows), F32),
-        in_specs=[pl.BlockSpec(memory_space=pl.ANY)],
+        in_specs=[pl.BlockSpec(memory_space=pltpu.VMEM)],
         out_specs=pl.BlockSpec(memory_space=pltpu.VMEM),
         scratch_shapes=[
-            pltpu.VMEM((tables, quarter, rows), BF16),
-            pltpu.VMEM((tables, 3, quarter, rows), BF16),
-            pltpu.SemaphoreType.DMA((tables,)),
-            pltpu.SemaphoreType.DMA((3 * tables,)),
-            pltpu.SemaphoreType.DMA((3 * tables,)),
+            pltpu.VMEM((tables, 2, quarter // 2, rows), BF16),
+            pltpu.VMEM((tables, 2, quarter // 2, rows), BF16),
+            pltpu.VMEM((tables, 2, quarter, rows), BF16),
+            pltpu.SemaphoreType.DMA((2, 6 * tables)),
         ],
         compiler_params=pltpu.CompilerParams(collective_id=2, has_side_effects=True),
         cost_estimate=pl.CostEstimate(flops=10**6, bytes_accessed=60 * 10**6, transcendentals=0),
@@ -557,13 +613,11 @@
     shards = lax.axis_size("table")
     groups = lax.axis_size("dp")
     slot_count = 8 * ((6 * item_count + 8 * shards - 1) // (8 * shards))
-    place, requests, items = make_index(
+    place, asked, items = make_index(
         jnp.transpose(shard_of, (2, 0, 1)), jnp.transpose(offsets, (2, 0, 1)), shards, slot_count, rows_dev
     )
-    asked = lax.all_to_all(requests, "table", split_axis=0, concat_axis=0, tiled=True).reshape(-1)
-    found = jnp.maximum(asked - 1, 0)
-    spots = jnp.where(asked > 0, asked - 1, rows)
-    (got,) = exchange(found, table.reshape(rows, width), shards, 0, "rows_out")
+    asked = asked.reshape(-1)
+    (got,) = exchange(asked, table.reshape(rows, width), shards, slot_count, 0, "rows_out")
     scale = 1.0 / math.sqrt(item_count * groups * shards)
     block_out, grad_embed, first_weights, second_weights, gains = block_pass(
         place.reshape(-1),
@@ -580,12 +634,13 @@
         items.reshape(-1),
         grad_embed,
         shards,
+        slot_count,
         1,
         "grads_out",
         (first_weights.reshape(tiles), second_weights.reshape(tiles), gains, scale),
     )
     totals = totals.reshape(-1, width)
-    dense = collect(spots, arrived.reshape(-1, width), rows)
+    dense = collect(asked, arrived.reshape(-1, width), rows, slot_count)
     table_grad = jnp.transpose(group_sum(dense), (0, 2, 1))
     block_out = block_out.reshape(sessions, length, width)
     return block_out, totals[:768], totals[768:1536], totals[1536], totals[1537], table_grad

time: 402 us -> 363 us (0.903)
  starting transfers between devices: 12.3 us -> 0 us
  Pallas kernels: 365 us -> 353 us
  waiting for transfers between devices: 6.53 us -> 0 us
  local copies, waits for them, and re-layouts: 12.6 us -> 6.65 us
    pallas_call x2, Pallas kernels: 271 us -> 248 us  [exchange(): pl.pallas_call(functools.partial(exchange_kernel, scale), out_shape=out_s...]
    pallas_call x2, Pallas kernels: 33.9 us -> 47.8 us  [the longest x1 25.8 us: collect(): pl.pallas_call(functools.partial(collect_kernel, ways, cap), out_shape=ja...]
    all_to_all x1 -> x0, starting transfers between devices: 12.3 us -> none  [on_device(): lax.all_to_all(requests, 'table', split_axis=0, concat_axis=0, tiled=True)]
    all_to_all x1 -> x0, waiting for transfers between devices: 6.53 us -> none  [on_device(): lax.all_to_all(requests, 'table', split_axis=0, concat_axis=0, tiled=True)]
  transfers between devices with their start and end apart: 1 -> 0, of which waited for: 1 -> 0; matrix products, arithmetic and copies ran while one was open for 1% -> 0% of each run, Pallas kernels for 0% -> 0%
where the time goes in v1:
time: 363 us; the launch traced here: 360 us
  Pallas kernels  353 us (97%)
  local copies, waits for them, and re-layouts  6.65 us (2%)
    pallas_call x2, Pallas kernels, exchange(): pl.pallas_call(functools.partial(exchange_kernel, scale), out_shape=out_s...  248 us
    pallas_call x1, Pallas kernels, group_sum(): pl.pallas_call(group_sum_kernel, out_shape=jax.ShapeDtypeStruct((tables,...  34.5 us
    pallas_call x1, Pallas kernels, collect(): pl.pallas_call(functools.partial(collect_kernel, ways, cap), out_shape=ja...  25.8 us
    pallas_call x1, Pallas kernels, block_pass(): pl.pallas_call(functools.partial(block_kernel, length), out_shape=[jax.Sh...  23 us
    pallas_call x1, Pallas kernels, make_index(): pl.pallas_call(functools.partial(index_kernel, cap, rows_dev), out_shape=...  22.1 us

profile of v1, /device:TPU:2, one launch (start us, length us, event | category | flops | bytes accessed | tf_op | source)
XLA Modules:
  0.0 360.2 jit_solution(9185678243305564400)
XLA Ops:
  0.6 22.1 %index.1 = (s32[24,2,128]{2,1,0:T(2,128)}, s32[64,2,128]{2,1,0:T(2,128)}, s32[64,2,128]{2,1,0:T(2,128)}) custom-call(s32[3,8,200]{2,1,0:T(8,128)} %bitcast.32, s32[3,8,200]{2,1,0:T(8,128)} %bitcast.33), custom_call_target="tpu_custom_call" | custom-call | flops 1000000000 | bytes 1000000 | tf_op jit(solution)/shard_map/index/pallas_call | solution.py:95
  22.7 116.9 %rows_out.1 = bf16[64,152,256]{2,1,0:T(8,128)(2,1)} custom-call(s32[16384]{0:T(1024)} %bitcast.26, bf16[6144,256]{1,0:T(8,128)(2,1)} %bitcast.21), custom_call_target="tpu_custom_call" | custom-call | flops 10000000 | bytes 100000000 | tf_op jit(solution)/shard_map/rows_out/pallas_call | solution.py:519
  139.6 23.0 %block_pass.1 = (bf16[1600,256]{1,0:T(8,128)(2,1)}, bf16[1600,256]{1,0:T(8,128)(2,1)}, f32[768,256]{1,0:T(8,128)}, f32[768,256]{1,0:T(8,128)}, f32[8,256]{1,0:T(8,128)}) custom-call(s32[6144]{0:T(1024)} %bitcast.37, bf16[9728,256]{1,0:T(8,128)(2,1)} %bitcast.20, bf16[768,256]{1,0:T(8,128)(2,1)} %w1_ref.1, f32[1,256]{1,0:T(1,128)} %bitcast.34, ...), custom_call_target="tpu_custom_call" | custom-call | flops 4000000000 | bytes 30000000 | tf_op jit(solution)/shard_map/block_pass/pallas_call | solution.py:248
  162.6 130.7 %grads_out.1 = (bf16[64,152,256]{2,1,0:T(8,128)(2,1)}, f32[4,4,16,8,256]{4,3,2,1,0:T(8,128)}) custom-call(s32[16384]{0:T(1024)} %bitcast.28, bf16[1600,256]{1,0:T(8,128)(2,1)} %get-tuple-element.20.table_ref, f32[96,8,256]{2,1,0:T(8,128)} %bitcast.24, f32[96,8,256]{2,1,0:T(8,128)} %bitcast.25, f32[8,256]{1,0:T(8,128)} %get-tuple-element.23.rest_2_), custom_call_target="tpu_custom_call" | custom-call | flops 10000000 | bytes 100000000 | tf_op jit(solution)/shard_map/grads_out/pallas_call | solution.py:519
  293.3 2.6 fusion.1
  295.9 1.3 fusion
  297.2 25.8 %collect.1.dense_ref = bf16[3,256,2048]{2,1,0:T(8,128)(2,1)} custom-call(s32[16384]{0:T(1024)} %bitcast.27, bf16[9728,256]{1,0:T(8,128)(2,1)} %bitcast.19), custom_call_target="tpu_custom_call" | custom-call | flops 10000000 | bytes 60000000 | tf_op jit(solution)/shard_map/collect/pallas_call | solution.py:305
  323.0 34.5 %group_sum.1 = f32[3,64,2048]{2,1,0:T(8,128)} custom-call(bf16[3,256,2048]{2,1,0:T(8,128)(2,1)} %collect.1.dense_ref), custom_call_target="tpu_custom_call" | custom-call | flops 1000000 | bytes 60000000 | tf_op jit(solution)/shard_map/group_sum/pallas_call | solution.py:590
  357.5 2.7 copy.15

commit v2 on v1

--- a/solution.py
+++ b/solution.py
@@ -14,7 +14,6 @@
 GELU_K = 0.044715
 PITCH = 256
 EDGE = 8
-GROUP = 8
 AXES = (("dp", 4, 1), ("table", 4, 16), ("table", 8, 2), ("table", 2, 1))
 
 
@@ -28,7 +27,7 @@
     return (output, slope)
 
 
-def index_kernel(cap, rows_dev, sh_ref, off_ref, place_ref, asked_ref, item_ref, req_ref, send, recv):
+def index_kernel(cap, rows_dev, sh_ref, off_ref, place_ref, asked_ref, lists_ref, req_ref, item_ref, send, recv, list_send, list_recv):
     tables, sessions, length = sh_ref.shape
     shards = asked_ref.shape[0]
     me = lax.axis_index("table")
@@ -84,20 +83,37 @@
 
     lax.fori_loop(1, shards, ask, 0)
     asked_ref[me] = req_ref[me]
+    ymine, zmine, cmine = spot()
+    zsize, plane = lists_ref.shape[:2]
+
+    def tell(step, _):
+        z = lax.rem(zmine + step, zsize)
+        for k in range(plane):
+            source = item_ref.at[device_at(*plane_spot(k), z)]
+            remote(source, lists_ref.at[zmine, k], list_send, list_recv, {"table": device_at(ymine, cmine, z)}).start()
+        return 0
+
+    lax.fori_loop(1, zsize, tell, 0)
+    for k in range(plane):
+        lists_ref[zmine, k] = item_ref[device_at(*plane_spot(k), zmine)]
     many = pl.ds(0, shards - 1)
     remote(req_ref.at[many], asked_ref.at[many], send, recv, {"table": visit(1)}).wait()
+    many = item_ref.at[pl.ds(0, shards - plane)]
+    remote(many, many, list_send, list_recv, {"table": visit(1)}).wait()
 
 
 def make_index(sh, off, shards, cap, rows_dev):
     tables, sessions, _ = sh.shape
     block = jax.ShapeDtypeStruct((shards, 2, 128), I32)
+    zsize = AXES[2][1]
+    lists = jax.ShapeDtypeStruct((zsize, shards // zsize, 2, 128), I32)
     vmem = pl.BlockSpec(memory_space=pltpu.VMEM)
     return pl.pallas_call(
         functools.partial(index_kernel, cap, rows_dev),
-        out_shape=(jax.ShapeDtypeStruct((tables * sessions, 2, 128), I32), block, block),
+        out_shape=(jax.ShapeDtypeStruct((tables * sessions, 2, 128), I32), block, lists),
         in_specs=[vmem] * 2,
         out_specs=[vmem] * 3,
-        scratch_shapes=[pltpu.VMEM((shards, 2, 128), I32), pltpu.SemaphoreType.DMA, pltpu.SemaphoreType.DMA],
+        scratch_shapes=[pltpu.VMEM((shards, 2, 128), I32)] * 2 + [pltpu.SemaphoreType.DMA] * 4,
         compiler_params=pltpu.CompilerParams(collective_id=3, has_side_effects=True),
         cost_estimate=pl.CostEstimate(flops=10**9, bytes_accessed=10**6, transcendentals=0),
         name="index",
@@ -339,25 +355,31 @@
     return y * ystride + z * zstride + c
 
 
+def spot():
+    me = lax.axis_index("table")
+    (_, _, ystride), (_, zsize, zstride), (_, csize, _) = AXES[1:]
+    return lax.div(me, ystride), lax.rem(lax.div(me, zstride), zsize), lax.rem(me, csize)
+
+
+def device_at(y, c, z):
+    return y * AXES[1][2] + z * AXES[2][2] + c
+
+
+def plane_spot(k):
+    return k // AXES[3][1], k % AXES[3][1]
+
+
 def remote(src, dst, send, recv, device):
     return pltpu.make_async_remote_copy(
         src_ref=src, dst_ref=dst, send_sem=send, recv_sem=recv, device_id=device, device_id_type=MESH
     )
 
 
-def exchange_kernel(scale, idx_ref, table_ref, *rest):
-    summing = scale is not None
-    if summing:
-        w1_ref, w2_ref, gains_ref, got_ref, out_ref, wide, stage, held, own_sem, sends, recv, *more = rest
-        part, r0, s0, r1, s1, r2, a2, a1, *sems = more
-    else:
-        got_ref, wide, stage, held, own_sem, sends, recv = rest
+def exchange_kernel(idx_ref, table_ref, got_ref, wide, stage, held, own_sem, send, recv):
     shards, cap, width = held.shape
     rows = table_ref.shape[0]
     me = lax.axis_index("table")
-    group = GROUP
     total = shards - 1
-
     barrier = pltpu.get_barrier_semaphore()
 
     def hello(step, _):
@@ -365,9 +387,6 @@
         return 0
 
     lax.fori_loop(1, shards, hello, 0)
-    if summing:
-        for step in range(1, AXES[0][1]):
-            pl.semaphore_signal(barrier, inc=1, device_id=peer_of(0, step)[2], device_id_type=MESH)
 
     def widened(c, _):
         at = pl.ds(pl.multiple_of(c * 64, 64), 64)
@@ -375,46 +394,7 @@
         return 0
 
     wide[0:EDGE, :] = jnp.zeros((EDGE, width), F32)
-
     lax.fori_loop(0, rows // 64, widened, 0)
-    if summing:
-        parts = [(w1_ref, w1_ref.shape[0]), (w2_ref, w2_ref.shape[0]), (gains_ref, 1)]
-        ysize, zcsize = part.shape[1:3]
-        block = 0
-        for ref, count in parts:
-            done = 0
-            while done < count:
-                many = min(count - done, zcsize - block % zcsize)
-                first = block % zcsize
-                row = ref[...][None] if ref is gains_ref else ref[done : done + many]
-                part[block // (ysize * zcsize), block // zcsize % ysize, first : first + many] = row
-                done, block = done + many, block + many
-        while block < part.shape[0] * ysize * zcsize:
-            many = zcsize - block % zcsize
-            empty = jnp.zeros((many,) + part.shape[3:], F32)
-            part[block // (ysize * zcsize), block // zcsize % ysize, block % zcsize :] = empty
-            block += many
-        ymine, zcmine = lax.div(me, zcsize), lax.rem(me, zcsize)
-        xmine = peer_of(0, 1)[0]
-        xpeers = [peer_of(0, step)[1:] for step in range(1, AXES[0][1])]
-        ypeers = [lax.rem(ymine + step, ysize) for step in range(1, ysize)]
-        ypeers = [(other, {"table": other * zcsize + zcmine}) for other in ypeers]
-        zcpeers = [lax.rem(zcmine + step, zcsize) for step in range(1, zcsize)]
-        zcpeers = [(other, {"table": ymine * zcsize + other}) for other in zcpeers]
-
-        def fan(stage, peers, src, dst):
-            send_sem, recv_sem = sems[2 * stage : 2 * stage + 2]
-            copies = [
-                remote(src(other), dst(n), send_sem.at[n], recv_sem.at[n], device)
-                for n, (other, device) in enumerate(peers)
-            ]
-            for copy in copies:
-                copy.start()
-            return copies
-
-        def landed(copies):
-            for copy in copies:
-                copy.wait_recv()
 
     def gather(step):
         dest = visit(step)
@@ -424,108 +404,251 @@
         held[step] = stage[...].astype(BF16)
 
     def post(step):
-        remote(
-            held.at[step],
-            got_ref.at[me],
-            sends.at[lax.div(step - 1, group)],
-            recv,
-            {"table": visit(step)},
-        ).start()
-
-    def sent(number, count):
-        ref = held.at[pl.ds(0, count)]
-        remote(ref, ref, sends.at[number], recv, {"table": visit(1)}).wait_send()
-
-    gather(0)
-    own = pltpu.make_async_copy(held.at[0], got_ref.at[me], own_sem)
+        remote(held.at[step], got_ref.at[me], send, recv, {"table": visit(step)}).start()
+
     gather(1)
-    pl.semaphore_wait(barrier, total + (AXES[0][1] - 1 if summing else 0))
-    own.start()
-    if summing:
-        flights = [fan(0, xpeers, lambda other: part.at[other], lambda n: r0.at[n])]
+    pl.semaphore_wait(barrier, total)
 
     def go(step, _):
         gather(step)
         post(step - 1)
         return 0
 
-    groups = -(-total // group)
-    for number in range(groups):
-        if summing and number >= 2:
-            sent(number - 2, group)
-        low, high = number * group + 2, min((number + 1) * group + 1, shards - 1)
-        lax.fori_loop(low, high + 1, go, 0)
-        if number == groups - 1:
-            post(shards - 1)
-        if summing and number >= 1:
-            for stage in range(number, number + 1) if number < groups - 1 else range(number, 6):
-                if stage > 5:
-                    continue
-                landed(flights[-1])
-                if stage == 1:
-                    s0[...] = sum([r0[n] for n in range(len(xpeers))], part[xmine])
-                    flights.append(fan(1, ypeers, lambda other: s0.at[other], lambda n: r1.at[n]))
-                elif stage == 2:
-                    s1[...] = sum([r1[n] for n in range(len(ypeers))], s0[ymine])
-                    flights.append(fan(2, zcpeers, lambda other: s1.at[other], lambda n: r2.at[n]))
-                elif stage == 3:
-                    a2[zcmine] = sum([r2[n] for n in range(len(zcpeers))], s1[zcmine]) * scale
-                    flights.append(fan(3, zcpeers, lambda _: a2.at[zcmine], lambda _: a2.at[zcmine]))
-                elif stage == 4:
-                    flights.append(fan(4, ypeers, lambda _: a2, lambda _: a1.at[ymine]))
-                    a1[ymine] = a2[...]
-                elif stage == 5:
-                    flights.append(fan(5, xpeers, lambda _: a1, lambda _: out_ref.at[xmine]))
-                    out_ref[xmine] = a1[...]
-    for number in range(groups):
-        if not summing or number >= groups - 2:
-            sent(number, min(group, total - number * group))
+    lax.fori_loop(2, shards, go, 0)
+    post(total)
+    gather(0)
+    own = pltpu.make_async_copy(held.at[0], got_ref.at[me], own_sem)
+    own.start()
     own.wait()
-    ref = held.at[pl.ds(0, total)]
-    remote(ref, got_ref.at[pl.ds(0, total)], sends.at[0], recv, {"table": visit(1)}).wait_recv()
-    if summing:
+    many = pl.ds(0, total)
+    remote(held.at[many], got_ref.at[many], send, recv, {"table": visit(1)}).wait()
+
+
+def exchange(idx, table, shards, cap, collective_id, name):
+    rows, width = table.shape
+    return pl.pallas_call(
+        exchange_kernel,
+        out_shape=jax.ShapeDtypeStruct((shards, cap, width), BF16),
+        in_specs=[pl.BlockSpec(memory_space=pltpu.SMEM), pl.BlockSpec(memory_space=pltpu.VMEM)],
+        out_specs=pl.BlockSpec(memory_space=pl.ANY),
+        scratch_shapes=[
+            pltpu.VMEM((rows + EDGE, width), F32),
+            pltpu.VMEM((cap, width), F32),
+            pltpu.VMEM((shards, cap, width), BF16),
+            pltpu.SemaphoreType.DMA,
+            pltpu.SemaphoreType.DMA,
+            pltpu.SemaphoreType.DMA,
+        ],
+        compiler_params=pltpu.CompilerParams(collective_id=collective_id, has_side_effects=True),
+        cost_estimate=pl.CostEstimate(flops=10**7, bytes_accessed=10**8, transcendentals=0),
+        name=name,
+    )(idx, table)
+
+
+def relay_kernel(
+    scale, idx_ref, table_ref, w1_ref, w2_ref, gains_ref, got_ref, out_ref,
+    blocks, wide, stage, held, own_sem, ring_send, ring_recv, send, recv,
+    part, r0, s0, r1, s1, r2, a2, a1, *sems,
+):
+    zsize, rows, width = blocks.shape
+    shards, cap, _ = held.shape
+    plane = shards // zsize
+    me = lax.axis_index("table")
+    ymine, zmine, cmine = spot()
+    parts = [(w1_ref, w1_ref.shape[0]), (w2_ref, w2_ref.shape[0]), (gains_ref, 1)]
+    ysize, zcsize = part.shape[1:3]
+    block = 0
+    for ref, count in parts:
+        done = 0
+        while done < count:
+            many = min(count - done, zcsize - block % zcsize)
+            first = block % zcsize
+            row = ref[...][None] if ref is gains_ref else ref[done : done + many]
+            part[block // (ysize * zcsize), block // zcsize % ysize, first : first + many] = row
+            done, block = done + many, block + many
+    while block < part.shape[0] * ysize * zcsize:
+        many = zcsize - block % zcsize
+        empty = jnp.zeros((many,) + part.shape[3:], F32)
+        part[block // (ysize * zcsize), block // zcsize % ysize, block % zcsize :] = empty
+        block += many
+    zcmine = lax.rem(me, zcsize)
+    xmine = peer_of(0, 1)[0]
+    xpeers = [peer_of(0, step)[1:] for step in range(1, AXES[0][1])]
+    ypeers = [lax.rem(ymine + step, ysize) for step in range(1, ysize)]
+    ypeers = [(other, {"table": other * zcsize + zcmine}) for other in ypeers]
+    zcpeers = [lax.rem(zcmine + step, zcsize) for step in range(1, zcsize)]
+    zcpeers = [(other, {"table": ymine * zcsize + other}) for other in zcpeers]
+
+    def fan(stage, peers, src, dst):
+        send_sem, recv_sem = sems[2 * stage : 2 * stage + 2]
+        copies = [
+            remote(src(other), dst(n), send_sem.at[n], recv_sem.at[n], device)
+            for n, (other, device) in enumerate(peers)
+        ]
+        for copy in copies:
+            copy.start()
+        return copies
+
+    def landed(copies):
+        for copy in copies:
+            copy.wait_recv()
+
+    barrier = pltpu.get_barrier_semaphore()
+    others = []
+    for dy in range(1, ysize):
+        for dc in range(AXES[3][1]):
+            y, c = lax.rem(ymine + dy, ysize), lax.rem(cmine + dc, AXES[3][1])
+            others.append({"table": device_at(y, c, zmine)})
+    known = [device for _, device in xpeers + zcpeers] + others
+    for device in known:
+        pl.semaphore_signal(barrier, inc=1, device_id=device, device_id_type=MESH)
+    wide[0:EDGE, :] = jnp.zeros((EDGE, width), F32)
+    pl.semaphore_wait(barrier, len(known))
+    right = {"table": device_at(ymine, cmine, lax.rem(zmine + 1, zsize))}
+    left = {"table": device_at(ymine, cmine, lax.rem(zmine + zsize - 1, zsize))}
+    far = zsize // 2
+    half = rows // 2
+
+    def ring(way, hop):
+        source = lax.rem(zmine + (zsize - hop if way == 0 else hop), zsize)
+        src, dst = table_ref if hop == 0 else blocks.at[source], blocks.at[source]
+        if hop == far - 1:
+            at = pl.ds(way * half, half)
+            src, dst = src.at[at], dst.at[at]
+        return remote(src, dst, ring_send.at[way, hop], ring_recv.at[way, hop], right if way == 0 else left)
+
+    copies = {(way, hop): ring(way, hop) for way in range(2) for hop in range(far)}
+    flights = [fan(0, xpeers, lambda other: part.at[other], lambda n: r0.at[n])]
+    for way in range(2):
+        copies[way, 0].start()
+
+    def serve(number, source, rows_ref):
+        def widened(c, _):
+            at = pl.ds(pl.multiple_of(c * 64, 64), 64)
+            wide[pl.ds(pl.multiple_of(EDGE + c * 64, EDGE), 64), :] = rows_ref[at, :].astype(F32)
+            return 0
+
+        lax.fori_loop(0, rows // 64, widened, 0)
+        origin = device_at(ymine, cmine, source)
+
+        def turned(step):
+            y, c = plane_spot(step)
+            return lax.rem(ymine + y, ysize), lax.rem(cmine + c, AXES[3][1])
+
+        def gather(step):
+            y, c = turned(step)
+            base = (source * plane + y * AXES[3][1] + c) * PITCH
+            for k in range(0, cap, 8):
+                rows8 = [wide[pl.ds(idx_ref[base + k + j], 1), :] for j in range(8)]
+                stage[k : k + 8, :] = jnp.concatenate(rows8, axis=0)
+            held[number * plane + step] = stage[...].astype(BF16)
+
+        def post(step):
+            y, c = turned(step)
+            remote(
+                held.at[number * plane + step], got_ref.at[origin], send, recv, {"table": device_at(y, c, zmine)}
+            ).start()
+
+        def go(step, _):
+            gather(step)
+            post(step - 1)
+            return 0
+
+        gather(1)
+        lax.fori_loop(2, plane, go, 0)
+        post(plane - 1)
+        gather(0)
+        own = pltpu.make_async_copy(held.at[number * plane], got_ref.at[origin], own_sem.at[number])
+        own.start()
+        return own
+
+    def sum_stage(stage_number):
         landed(flights[-1])
-        for copies in flights:
-            for copy in copies:
-                copy.wait_send()
-
-
-def exchange(idx, table, shards, cap, collective_id, name, sums=None):
+        if stage_number == 1:
+            s0[...] = sum([r0[n] for n in range(len(xpeers))], part[xmine])
+            flights.append(fan(1, ypeers, lambda other: s0.at[other], lambda n: r1.at[n]))
+        elif stage_number == 2:
+            s1[...] = sum([r1[n] for n in range(len(ypeers))], s0[ymine])
+            flights.append(fan(2, zcpeers, lambda other: s1.at[other], lambda n: r2.at[n]))
+        elif stage_number == 3:
+            a2[zcmine] = sum([r2[n] for n in range(len(zcpeers))], s1[zcmine]) * scale
+            flights.append(fan(3, zcpeers, lambda _: a2.at[zcmine], lambda _: a2.at[zcmine]))
+        elif stage_number == 4:
+            flights.append(fan(4, ypeers, lambda _: a2, lambda _: a1.at[ymine]))
+            a1[ymine] = a2[...]
+        elif stage_number == 5:
+            flights.append(fan(5, xpeers, lambda _: a1, lambda _: out_ref.at[xmine]))
+            out_ref[xmine] = a1[...]
+
+    locals_ = [serve(0, zmine, table_ref)]
+    number, done = 1, 0
+    for hop in range(1, far + 1):
+        if hop < far:
+            for way in range(2):
+                copies[way, hop - 1].wait_recv()
+                copies[way, hop].start()
+                source = lax.rem(zmine + (zsize - hop if way == 0 else hop), zsize)
+                locals_.append(serve(number, source, blocks.at[source]))
+                number += 1
+                if done < 5:
+                    done += 1
+                    sum_stage(done)
+        else:
+            while done < 5:
+                done += 1
+                sum_stage(done)
+            source = lax.rem(zmine + far, zsize)
+            for way in range(2):
+                copies[way, hop - 1].wait_recv()
+            locals_.append(serve(number, source, blocks.at[source]))
+    for copy in copies.values():
+        copy.wait_send()
+    for copy in locals_:
+        copy.wait()
+    many = pl.ds(0, shards - zsize)
+    remote(held.at[many], got_ref.at[many], send, recv, right).wait()
+    landed(flights[-1])
+    for flight in flights:
+        for copy in flight:
+            copy.wait_send()
+
+
+def relay(idx, table, shards, cap, w1, w2, gains, scale):
     rows, width = table.shape
-    any_space, vmem = pl.BlockSpec(memory_space=pl.ANY), pl.BlockSpec(memory_space=pltpu.VMEM)
-    out_shape = [jax.ShapeDtypeStruct((shards, cap, width), BF16)]
-    out_specs = [any_space]
+    (xsize, ysize, zsize), zcsize = [AXES[n][1] for n in range(3)], AXES[1][2]
+    tile = w1.shape[1:]
+    line, plane = (zcsize,) + tile, (ysize, zcsize) + tile
+    shapes = [(xsize,) + plane, (xsize - 1,) + plane, plane, (ysize - 1,) + line, line]
+    shapes += [(zcsize - 1,) + tile, line, plane]
+    dma = pltpu.SemaphoreType.DMA
     scratch = [
+        pltpu.VMEM((zsize, rows, width), BF16),
         pltpu.VMEM((rows + EDGE, width), F32),
         pltpu.VMEM((cap, width), F32),
         pltpu.VMEM((shards, cap, width), BF16),
-        pltpu.SemaphoreType.DMA,
-        pltpu.SemaphoreType.DMA((-(-(shards - 1) // GROUP),)),
-        pltpu.SemaphoreType.DMA,
+        dma((zsize,)),
+        dma((2, zsize // 2)),
+        dma((2, zsize // 2)),
+        dma,
+        dma,
     ]
-    operands, scale = [], None
-    if sums is not None:
-        *operands, scale = sums
-        xsize, ysize, zcsize = AXES[0][1], AXES[1][1], AXES[1][2]
-        tile = operands[0].shape[1:]
-        line, plane = (zcsize,) + tile, (ysize, zcsize) + tile
-        out_shape.append(jax.ShapeDtypeStruct((xsize,) + plane, F32))
-        out_specs.append(vmem)
-        shapes = [(xsize,) + plane, (xsize - 1,) + plane, plane, (ysize - 1,) + line, line]
-        shapes += [(zcsize - 1,) + tile, line, plane]
-        scratch += [pltpu.VMEM(shape, F32) for shape in shapes]
-        for size in (xsize, ysize, zcsize, zcsize, ysize, xsize):
-            scratch += [pltpu.SemaphoreType.DMA((size - 1,))] * 2
+    scratch += [pltpu.VMEM(shape, F32) for shape in shapes]
+    for size in (xsize, ysize, zcsize, zcsize, ysize, xsize):
+        scratch += [dma((size - 1,))] * 2
+    vmem = pl.BlockSpec(memory_space=pltpu.VMEM)
     return pl.pallas_call(
-        functools.partial(exchange_kernel, scale),
-        out_shape=out_shape,
-        in_specs=[pl.BlockSpec(memory_space=pltpu.SMEM)] + [vmem] * (1 + len(operands)),
-        out_specs=out_specs,
+        functools.partial(relay_kernel, scale),
+        out_shape=[
+            jax.ShapeDtypeStruct((shards, cap, width), BF16),
+            jax.ShapeDtypeStruct((xsize,) + plane, F32),
+        ],
+        in_specs=[pl.BlockSpec(memory_space=pltpu.SMEM)] + [vmem] * 4,
+        out_specs=[pl.BlockSpec(memory_space=pl.ANY), vmem],
         scratch_shapes=scratch,
-        compiler_params=pltpu.CompilerParams(collective_id=collective_id, has_side_effects=True),
+        compiler_params=pltpu.CompilerParams(collective_id=1, has_side_effects=True),
         cost_estimate=pl.CostEstimate(flops=10**7, bytes_accessed=10**8, transcendentals=0),
-        name=name,
-    )(idx, table, *operands)
+        name="grads_out",
+    )(idx, table, w1, w2, gains)
 
 
 def greet(steps):
@@ -613,11 +736,11 @@
     shards = lax.axis_size("table")
     groups = lax.axis_size("dp")
     slot_count = 8 * ((6 * item_count + 8 * shards - 1) // (8 * shards))
-    place, asked, items = make_index(
+    place, asked, lists = make_index(
         jnp.transpose(shard_of, (2, 0, 1)), jnp.transpose(offsets, (2, 0, 1)), shards, slot_count, rows_dev
     )
     asked = asked.reshape(-1)
-    (got,) = exchange(asked, table.reshape(rows, width), shards, slot_count, 0, "rows_out")
+    got = exchange(asked, table.reshape(rows, width), shards, slot_count, 0, "rows_out")
     scale = 1.0 / math.sqrt(item_count * groups * shards)
     block_out, grad_embed, first_weights, second_weights, gains = block_pass(
         place.reshape(-1),
@@ -630,14 +753,15 @@
         grad_out.reshape(item_count, width),
     )
     tiles = (-1, 8, width)
-    arrived, totals = exchange(
-        items.reshape(-1),
+    arrived, totals = relay(
+        lists.reshape(-1),
         grad_embed,
         shards,
         slot_count,
-        1,
-        "grads_out",
-        (first_weights.reshape(tiles), second_weights.reshape(tiles), gains, scale),
+        first_weights.reshape(tiles),
+        second_weights.reshape(tiles),
+        gains,
+        scale,
     )
     totals = totals.reshape(-1, width)
     dense = collect(asked, arrived.reshape(-1, width), rows, slot_count)

time: 363 us -> 342 us (0.942)
  Pallas kernels: 353 us -> 333 us
    pallas_call x2, Pallas kernels: 248 us -> 230 us  [the longest x1 124 us: exchange(): pl.pallas_call(exchange_kernel, out_shape=jax.ShapeDtypeStruct((shards, c...]
where the time goes in v2:
time: 342 us; the launch traced here: 340 us
  Pallas kernels  333 us (97%)
  local copies, waits for them, and re-layouts  6.65 us (2%)
    pallas_call x1, Pallas kernels, exchange(): pl.pallas_call(exchange_kernel, out_shape=jax.ShapeDtypeStruct((shards, c...  124 us
    pallas_call x1, Pallas kernels, relay(): pl.pallas_call(functools.partial(relay_kernel, scale), out_shape=[jax.Sha...  106 us
    pallas_call x1, Pallas kernels, group_sum(): pl.pallas_call(group_sum_kernel, out_shape=jax.ShapeDtypeStruct((tables,...  32.5 us
    pallas_call x1, Pallas kernels, collect(): pl.pallas_call(functools.partial(collect_kernel, ways, cap), out_shape=ja...  24.6 us
    pallas_call x1, Pallas kernels, block_pass(): pl.pallas_call(functools.partial(block_kernel, length), out_shape=[jax.Sh...  23 us
    pallas_call x1, Pallas kernels, make_index(): pl.pallas_call(functools.partial(index_kernel, cap, rows_dev), out_shape=...  22.1 us

profile of v2, /device:TPU:2, one launch (start us, length us, event | category | flops | bytes accessed | tf_op | source)
XLA Modules:
  0.0 339.9 jit_solution(14589563804929227581)
XLA Ops:
  0.6 22.1 %index.1 = (s32[24,2,128]{2,1,0:T(2,128)}, s32[64,2,128]{2,1,0:T(2,128)}, s32[8,8,2,128]{3,2,1,0:T(2,128)}) custom-call(s32[3,8,200]{2,1,0:T(8,128)} %bitcast.32, s32[3,8,200]{2,1,0:T(8,128)} %bitcast.33), custom_call_target="tpu_custom_call" | custom-call | flops 1000000000 | bytes 1000000 | tf_op jit(solution)/shard_map/index/pallas_call | solution.py:111
  22.7 124.2 %rows_out.1 = bf16[64,152,256]{2,1,0:T(8,128)(2,1)} custom-call(s32[16384]{0:T(1024)} %bitcast.26, bf16[6144,256]{1,0:T(8,128)(2,1)} %bitcast.21), custom_call_target="tpu_custom_call" | custom-call | flops 10000000 | bytes 100000000 | tf_op jit(solution)/shard_map/rows_out/pallas_call | solution.py:429
  146.9 23.0 %block_pass.1 = (bf16[1600,256]{1,0:T(8,128)(2,1)}, bf16[1600,256]{1,0:T(8,128)(2,1)}, f32[768,256]{1,0:T(8,128)}, f32[768,256]{1,0:T(8,128)}, f32[8,256]{1,0:T(8,128)}) custom-call(s32[6144]{0:T(1024)} %bitcast.37, bf16[9728,256]{1,0:T(8,128)(2,1)} %bitcast.20, bf16[768,256]{1,0:T(8,128)(2,1)} %w1_ref.1, f32[1,256]{1,0:T(1,128)} %bitcast.34, ...), custom_call_target="tpu_custom_call" | custom-call | flops 4000000000 | bytes 30000000 | tf_op jit(solution)/shard_map/block_pass/pallas_call | solution.py:264
  169.9 106.2 %grads_out.1 = (bf16[64,152,256]{2,1,0:T(8,128)(2,1)}, f32[4,4,16,8,256]{4,3,2,1,0:T(8,128)}) custom-call(s32[16384]{0:T(1024)} %bitcast.28, bf16[1600,256]{1,0:T(8,128)(2,1)} %get-tuple-element.20.table_ref, f32[96,8,256]{2,1,0:T(8,128)} %bitcast.24, f32[96,8,256]{2,1,0:T(8,128)} %bitcast.25, f32[8,256]{1,0:T(8,128)} %get-tuple-element.23.gains_ref), custom_call_target="tpu_custom_call" | custom-call | flops 10000000 | bytes 100000000 | tf_op jit(solution)/shard_map/grads_out/pallas_call | solution.py:639
  276.1 2.6 fusion.1
  278.7 1.3 fusion
  280.1 24.6 %collect.1.dense_ref = bf16[3,256,2048]{2,1,0:T(8,128)(2,1)} custom-call(s32[16384]{0:T(1024)} %bitcast.27, bf16[9728,256]{1,0:T(8,128)(2,1)} %bitcast.19), custom_call_target="tpu_custom_call" | custom-call | flops 10000000 | bytes 60000000 | tf_op jit(solution)/shard_map/collect/pallas_call | solution.py:321
  304.7 32.5 %group_sum.1 = f32[3,64,2048]{2,1,0:T(8,128)} custom-call(bf16[3,256,2048]{2,1,0:T(8,128)(2,1)} %collect.1.dense_ref), custom_call_target="tpu_custom_call" | custom-call | flops 1000000 | bytes 60000000 | tf_op jit(solution)/shard_map/group_sum/pallas_call | solution.py:713
  337.2 2.7 copy.15

commit v3 on v2

--- a/solution.py
+++ b/solution.py
@@ -581,26 +581,20 @@
             out_ref[xmine] = a1[...]
 
     locals_ = [serve(0, zmine, table_ref)]
-    number, done = 1, 0
     for hop in range(1, far + 1):
-        if hop < far:
-            for way in range(2):
-                copies[way, hop - 1].wait_recv()
+        sources = [lax.rem(zmine + (zsize - hop if way == 0 else hop), zsize) for way in range(2)]
+        for way in range(2):
+            copies[way, hop - 1].wait_recv()
+            if hop < far:
                 copies[way, hop].start()
-                source = lax.rem(zmine + (zsize - hop if way == 0 else hop), zsize)
-                locals_.append(serve(number, source, blocks.at[source]))
-                number += 1
-                if done < 5:
-                    done += 1
-                    sum_stage(done)
-        else:
-            while done < 5:
-                done += 1
-                sum_stage(done)
-            source = lax.rem(zmine + far, zsize)
-            for way in range(2):
-                copies[way, hop - 1].wait_recv()
-            locals_.append(serve(number, source, blocks.at[source]))
+        if hop > 1:
+            sum_stage(hop)
+        for way in range(2 if hop < far else 1):
+            locals_.append(serve(2 * hop - 1 + way, sources[way], blocks.at[sources[way]]))
+        if hop == 1:
+            sum_stage(1)
+    for stage_number in range(far + 1, 6):
+        sum_stage(stage_number)
     for copy in copies.values():
         copy.wait_send()
     for copy in locals_:

time: 342 us -> 357 us (1.044)
  Pallas kernels: 333 us -> 346 us
    pallas_call x1, Pallas kernels: 106 us -> 120 us  [relay(): pl.pallas_call(functools.partial(relay_kernel, scale), out_shape=[jax.Sha...]
where the time goes in v3:
time: 357 us; the launch traced here: 353 us
  Pallas kernels  346 us (97%)
  local copies, waits for them, and re-layouts  6.65 us (2%)
    pallas_call x1, Pallas kernels, exchange(): pl.pallas_call(exchange_kernel, out_shape=jax.ShapeDtypeStruct((shards, c...  124 us
    pallas_call x1, Pallas kernels, relay(): pl.pallas_call(functools.partial(relay_kernel, scale), out_shape=[jax.Sha...  120 us
    pallas_call x1, Pallas kernels, group_sum(): pl.pallas_call(group_sum_kernel, out_shape=jax.ShapeDtypeStruct((tables,...  32.2 us
    pallas_call x1, Pallas kernels, collect(): pl.pallas_call(functools.partial(collect_kernel, ways, cap), out_shape=ja...  24.5 us
    pallas_call x1, Pallas kernels, block_pass(): pl.pallas_call(functools.partial(block_kernel, length), out_shape=[jax.Sh...  23 us
    pallas_call x1, Pallas kernels, make_index(): pl.pallas_call(functools.partial(index_kernel, cap, rows_dev), out_shape=...  22.1 us

profile of v3, /device:TPU:2, one launch (start us, length us, event | category | flops | bytes accessed | tf_op | source)
XLA Modules:
  0.0 352.8 jit_solution(6881064314301022990)
XLA Ops:
  0.6 22.1 %index.1 = (s32[24,2,128]{2,1,0:T(2,128)}, s32[64,2,128]{2,1,0:T(2,128)}, s32[8,8,2,128]{3,2,1,0:T(2,128)}) custom-call(s32[3,8,200]{2,1,0:T(8,128)} %bitcast.32, s32[3,8,200]{2,1,0:T(8,128)} %bitcast.33), custom_call_target="tpu_custom_call" | custom-call | flops 1000000000 | bytes 1000000 | tf_op jit(solution)/shard_map/index/pallas_call | solution.py:111
  22.7 124.2 %rows_out.1 = bf16[64,152,256]{2,1,0:T(8,128)(2,1)} custom-call(s32[16384]{0:T(1024)} %bitcast.26, bf16[6144,256]{1,0:T(8,128)(2,1)} %bitcast.21), custom_call_target="tpu_custom_call" | custom-call | flops 10000000 | bytes 100000000 | tf_op jit(solution)/shard_map/rows_out/pallas_call | solution.py:429
  146.9 23.0 %block_pass.1 = (bf16[1600,256]{1,0:T(8,128)(2,1)}, bf16[1600,256]{1,0:T(8,128)(2,1)}, f32[768,256]{1,0:T(8,128)}, f32[768,256]{1,0:T(8,128)}, f32[8,256]{1,0:T(8,128)}) custom-call(s32[6144]{0:T(1024)} %bitcast.37, bf16[9728,256]{1,0:T(8,128)(2,1)} %bitcast.20, bf16[768,256]{1,0:T(8,128)(2,1)} %w1_ref.1, f32[1,256]{1,0:T(1,128)} %bitcast.34, ...), custom_call_target="tpu_custom_call" | custom-call | flops 4000000000 | bytes 30000000 | tf_op jit(solution)/shard_map/block_pass/pallas_call | solution.py:264
  169.9 119.6 %grads_out.1 = (bf16[64,152,256]{2,1,0:T(8,128)(2,1)}, f32[4,4,16,8,256]{4,3,2,1,0:T(8,128)}) custom-call(s32[16384]{0:T(1024)} %bitcast.28, bf16[1600,256]{1,0:T(8,128)(2,1)} %get-tuple-element.20.table_ref, f32[96,8,256]{2,1,0:T(8,128)} %bitcast.24, f32[96,8,256]{2,1,0:T(8,128)} %bitcast.25, f32[8,256]{1,0:T(8,128)} %get-tuple-element.23.gains_ref), custom_call_target="tpu_custom_call" | custom-call | flops 10000000 | bytes 100000000 | tf_op jit(solution)/shard_map/grads_out/pallas_call | solution.py:633
  289.5 2.6 fusion.1
  292.1 1.3 fusion
  293.5 24.5 %collect.1.dense_ref = bf16[3,256,2048]{2,1,0:T(8,128)(2,1)} custom-call(s32[16384]{0:T(1024)} %bitcast.27, bf16[9728,256]{1,0:T(8,128)(2,1)} %bitcast.19), custom_call_target="tpu_custom_call" | custom-call | flops 10000000 | bytes 60000000 | tf_op jit(solution)/shard_map/collect/pallas_call | solution.py:321
  318.0 32.2 %group_sum.1 = f32[3,64,2048]{2,1,0:T(8,128)} custom-call(bf16[3,256,2048]{2,1,0:T(8,128)(2,1)} %collect.1.dense_ref), custom_call_target="tpu_custom_call" | custom-call | flops 1000000 | bytes 60000000 | tf_op jit(solution)/shard_map/group_sum/pallas_call | solution.py:707
  350.1 2.7 copy.15
